TPU v7x, 32 devices: a whole 2x2x4 slice. The times are simulated.
32 devices in a mesh: frames: 4 (over y, core), bricks: 8 (over z, x).
Axes of the slice: x: 2, y: 2, z: 4, core: 2. Of those that a mesh axis runs over, the one named last changes fastest.
Arguments:
- positions: float32 [3, 8, 16384], P(None, 'frames', 'bricks'), may hold values from 0 to 1
- counts: int32 [8, 8], P('frames'), may hold values from 1 to 2048, as said below
- kvec_x: int32 [128], replicated, may hold values from 1 to 64
- kvec_y: int32 [128], replicated, may hold values from 1 to 64
- kvec_z: int32 [8], replicated, may hold values from 1 to 64
Outputs:
- spectrum: float32 [128, 128, 8, 128], P('bricks', 'frames')
Inputs may be any that keep to these rules, and one draw needn't show every extreme that they name: `counts`: in every frame one brick holds exactly 2048 live atoms; the others hold 1 to 2048.
All inputs are finite; a program needn't handle non-finite values.
Results may differ from a plain program's by a relative error of at most 0.0033.
Values sent between devices are 32-bit elements; how exact they have to be, the bound alone decides.
No kernel may reach another device: no remote copies, remote signals or barrier semaphores. Data moves between devices by JAX's collectives and lax.ppermute only.
A program may use at most 64 MiB of HBM per device.

v0:
```python
import functools
import math

import jax
import jax.numpy as jnp
import numpy as np
from jax import lax
from jax.experimental import pallas as pl
from jax.experimental.pallas import tpu as pltpu
from jax.sharding import PartitionSpec as P

NW = 128
KMAX = 64
LANES = 128
UNIT = 4
PAIRS = 2
BIG = 8

def _fit(fun, degree):
    nodes = 0.125 * (1.0 + np.cos(np.pi * (np.arange(64) + 0.5) / 64))
    series = np.polynomial.chebyshev.Chebyshev.fit(nodes, fun(np.sqrt(nodes)), degree, domain=[0.0, 0.25])
    return [float(c) for c in series.convert(kind=np.polynomial.Polynomial).coef]


COS_C = _fit(lambda f: math.sqrt(2.0) * np.cos(np.pi * f), 4)
SIN_C = _fit(lambda f: math.sqrt(2.0) * np.sin(np.pi * f) / f, 4)


def _poly(coefs, u):
    acc = coefs[-1] * u + coefs[-2]
    for c in coefs[-3::-1]:
        acc = acc * u + c
    return acc


def cis(turns):
    f = turns - jnp.round(turns)
    u = f * f
    half_c = _poly(COS_C, u)
    half_s = _poly(SIN_C, u) * f
    return 1.0 - half_s * half_s, half_s * half_c


def density_kernel(ids, first, last, groups, n_x, n_z, share, *refs):
    n_args = 4 if first else 1 if last else 0
    args, refs = refs[:n_args], refs[n_args:]
    left_ref, right_ref, row_ref, arg_sem = refs[-4:]
    refs = refs[:-4]
    if not first:
        (pos_ref, prod_in, kb_ref, counts_ref), refs = refs[:4], refs[4:]
    n_local = min(n_args, 3)
    outs, local = refs[: len(refs) - n_local], refs[len(refs) - n_local :]
    if first:
        local = (*local, outs[3])
    copies = [
        pltpu.make_async_copy(args[i], local[i], arg_sem.at[i]) for i in range(n_args)
    ]
    for copy in copies:
        copy.start()
    if first:
        counts_ref, pos_ref, kb_ref = local[0], local[3], outs[1]
    rows = n_x * n_z
    n_shards, _, frames_here, capacity = pos_ref.shape
    brick = lax.axis_index("bricks")
    lane = lax.broadcasted_iota(jnp.int32, (n_z, LANES), 1)

    if first:
        kx_ref, kz_ref = local[1:3]
        copies[0].wait()
        for frame in range(frames_here):
            for at in range(counts_ref.shape[1]):
                outs[2][frame, at] = counts_ref[frame, at]
        copies[1].wait()
        copies[2].wait()
        for row in range(n_x + n_z + 16):
            if row < n_x:
                k = kx_ref[brick * n_x + row].astype(jnp.float32)
            elif row < n_x + n_z:
                k = kz_ref[row - n_x].astype(jnp.float32)
            else:
                q = row - n_x - n_z
                k = float(q + 1 if q < 8 else 8 * (q - 7))
            kb_ref[row : row + 1, :] = jnp.full((1, LANES), k, jnp.float32)
        copies[3].wait()

    for frame in range(frames_here):
        counts = [counts_ref[frame, brick ^ d] for d in ids]
        starts = [jnp.int32(0)]
        for count in counts:
            starts.append(starts[-1] + (count + LANES - 1) // LANES)

        def build(item, slot, frame=frame, counts=counts, starts=starts):
            shard, start, count = jnp.int32(0), starts[0], counts[0]
            for s in range(1, n_shards):
                later = item >= starts[s]
                shard = jnp.where(later, s, shard)
                start = jnp.where(later, starts[s], start)
                count = jnp.where(later, counts[s], count)
            offset = (item - start) * LANES
            where = pl.ds(pl.multiple_of(jnp.minimum(offset, capacity - LANES), LANES), LANES)
            x = pos_ref[shard, 0, pl.ds(frame, 1), where]
            y = pos_ref[shard, 1, pl.ds(frame, 1), where]
            z = pos_ref[shard, 2, pl.ds(frame, 1), where]
            cx, sx = cis(kb_ref[0:n_x, :] * x)
            cz, sz = cis(kb_ref[n_x : n_x + n_z, :] * z)
            cy, sy = cis(kb_ref[n_x + n_z : n_x + n_z + 16, :] * y)
            live = lane + offset < count
            cz = jnp.where(live, cz, 0.0)
            sz = jnp.where(live, sz, 0.0)
            to = pl.ds(pl.multiple_of(item * LANES, LANES), LANES)
            half = n_x + 8
            base = slot * 2 * half
            row_ref[base : base + half, :] = jnp.concatenate([cx, cy[8:16]], axis=0)
            row_ref[base + half : base + 2 * half, :] = jnp.concatenate([sx, sy[8:16]], axis=0)

            def spread(q):
                return (
                    row_ref[pl.ds(base + q, 8, stride=0), :],
                    row_ref[pl.ds(base + half + q, 8, stride=0), :],
                )

            for i in range(0, n_x, 2):
                re, im = [], []
                for q in (i, i + 1):
                    a, b = spread(q)
                    re.append(a * cz - b * sz)
                    im.append(b * cz + a * sz)
                at = i * n_z
                left_ref[at : at + 2 * n_z, to] = jnp.concatenate(re, axis=0).astype(jnp.bfloat16)
                at += rows
                left_ref[at : at + 2 * n_z, to] = jnp.concatenate(im, axis=0).astype(jnp.bfloat16)
            ce, se = cy[0:8], sy[0:8]
            re, im = [ce], [se]
            for q in range(7):
                a, b = spread(n_x + q)
                re.append(a * ce - b * se)
                im.append(b * ce + a * se)
            for q in range(0, 8, 2):
                right_ref[8 * q : 8 * q + 16, to] = jnp.concatenate(re[q : q + 2], axis=0).astype(jnp.bfloat16)
                right_ref[KMAX + 8 * q : KMAX + 8 * q + 16, to] = jnp.concatenate(im[q : q + 2], axis=0).astype(jnp.bfloat16)

        def build_unit(unit, carry, build=build):
            for g in range(UNIT):
                build(unit * UNIT + g, g)
            return carry

        units = (starts[-1] + UNIT - 1) // UNIT
        lax.fori_loop(0, units, build_unit, 0)
        prod_ref = outs[0].at[frame] if not last else outs[-1].at[frame]
        prod_ref[...] = jnp.zeros(prod_ref.shape, jnp.float32) if first else prod_in[frame]

        def multiply(width):
            def step(base):
                where = pl.ds(pl.multiple_of(base, UNIT * LANES), width)
                prod_ref[...] += lax.dot_general(
                    left_ref[:, where],
                    right_ref[:, where],
                    (((1,), (1,)), ((), ())),
                    preferred_element_type=jnp.float32,
                )

            return step

        wide = multiply(BIG * UNIT * LANES)
        full = units // BIG

        def wide_step(i, carry, wide=wide):
            wide(i * (BIG * UNIT * LANES))
            return carry

        lax.fori_loop(0, full, wide_step, 0)
        for rest in range(1, BIG):

            @pl.when(units - full * BIG == rest)
            def _(rest=rest, multiply=multiply, full=full):
                multiply(rest * UNIT * LANES)(full * (BIG * UNIT * LANES))

    if last:
        copies[0].wait()
        send_own_rows(outs, groups, rows, share, frames_here, local[0])


def send_own_rows(outs, groups, rows, share, frames_here, ky_ref):
    prods = outs[-1]
    width = groups * share
    group = lax.axis_index("frames")
    column = lax.broadcasted_iota(jnp.int32, (1, width), 1)
    parts = [
        jnp.where(column == dest * share + j, ky_ref[(group ^ dest) * share + j], 0)
        for dest in range(groups)
        for j in range(share)
    ]
    while len(parts) > 1:
        parts = [sum(parts[i : i + 2][1:], parts[i]) for i in range(0, len(parts), 2)]
    wanted = parts[0]
    ks = lax.broadcasted_iota(jnp.int32, (KMAX, width), 0) + 1
    hot = jnp.where(ks == wanted, 1.0, 0.0).astype(jnp.bfloat16)
    none = jnp.zeros_like(hot)
    hot = jnp.concatenate(
        [jnp.concatenate([hot, none], axis=1), jnp.concatenate([none, hot], axis=1)], axis=0
    )
    hot = jnp.concatenate([hot, hot, hot], axis=0)
    first_half = lax.broadcasted_iota(jnp.int32, (rows, 2 * KMAX), 1) < KMAX
    for frame in range(frames_here):
        top = prods[frame, 0:rows, :]
        low = pltpu.roll(prods[frame, rows : 2 * rows, :], KMAX, 1)
        terms = jnp.where(first_half, top - low, -(top + low))
        hi = terms.astype(jnp.bfloat16)
        rest = terms - hi.astype(jnp.float32)
        mid = rest.astype(jnp.bfloat16)
        tail = (rest - mid.astype(jnp.float32)).astype(jnp.bfloat16)
        split = jnp.concatenate([hi, mid, tail], axis=1)
        picked = lax.dot_general(
            hot, split, (((0,), (1,)), ((), ())), preferred_element_type=jnp.float32
        )
        for part in range(2):
            for dest in range(groups):
                at = part * width + dest * share
                to = (frame * 2 + part) * share
                outs[dest][to : to + share, :] = picked[at : at + share, :]


def dft_table(table_ref, frames_total, atoms):
    weights = [0.5 - 0.5 * math.cos(2.0 * math.pi * (t + 0.5) / frames_total) for t in range(frames_total)]
    scale = 1.0 / math.sqrt(atoms * sum(w * w for w in weights))
    shape = (2 * frames_total, NW)
    row = lax.broadcasted_iota(jnp.int32, shape, 0)
    time = row // 2
    real = row % 2 == 0
    freq = lax.broadcasted_iota(jnp.int32, shape, 1)
    window = 0.5 - 0.5 * cis((time.astype(jnp.float32) + 0.5) / frames_total)[0]
    c, s = cis((time * freq % NW).astype(jnp.float32) / NW)
    cw, sw = scale * window * c, scale * window * s
    full = jnp.concatenate([jnp.where(real, cw, sw), jnp.where(real, -sw, cw)], axis=1)
    hi = full.astype(jnp.bfloat16)
    lo = (full - hi.astype(jnp.float32)).astype(jnp.bfloat16)
    none = jnp.zeros_like(hi)
    size = 2 * frames_total
    for split, part in enumerate((hi, lo, hi)):
        at = split * 2 * size
        table_ref[at : at + size, :] = jnp.concatenate([part, none], axis=1)
        table_ref[at + size : at + 2 * size, :] = jnp.concatenate([none, part], axis=1)


def spectrum_kernel(groups, share, chunk, n_x, n_z, frames_total, atoms, *refs):
    srcs = refs[:groups]
    out_hbm, out_ref, all_ref, table_ref, sem = refs[groups:]
    block = srcs[0].shape[0]
    terms = groups * block // share
    rows = n_x * n_z
    for distance in range(groups):
        at = pl.multiple_of((lax.axis_index("frames") ^ distance) * block, block)
        all_ref[pl.ds(at, block), :] = srcs[distance][...]
    dft_table(table_ref, frames_total, atoms)

    copies = []
    for base in range(0, share, chunk):
        for first in range(base, base + chunk, 2 * PAIRS):
            stacks = []
            for j in range(first, first + 2 * PAIRS, 2):
                x = jnp.concatenate(
                    [all_ref[pl.ds(j + q, terms, stride=share), :] for q in range(2)], axis=0
                )
                hi = x.astype(jnp.bfloat16)
                lo = (x - hi.astype(jnp.float32)).astype(jnp.bfloat16)
                stacks.append(jnp.concatenate([hi, hi, lo], axis=0))
            y = lax.dot_general(
                jnp.concatenate(stacks, axis=1),
                table_ref[...],
                (((0,), (0,)), ((), ())),
                preferred_element_type=jnp.float32,
            )
            for q in range(2 * PAIRS):
                own = y[q // 2 * rows : (q // 2 + 1) * rows]
                at = q % 2 * 2 * NW
                re, im = own[:, at : at + NW], own[:, at + NW : at + 2 * NW]
                out_ref[:, first + q] = (re * re + im * im).reshape(n_x, n_z, NW)
        part = pl.ds(base, chunk)
        copies.append(
            pltpu.make_async_copy(
                out_ref.at[:, part], out_hbm.at[:, part], sem.at[base // chunk]
            )
        )
        copies[-1].start()
    for copy in copies:
        copy.wait()


def swap(value, axis, size, distance):
    return lax.ppermute(value, axis, [(i, i ^ distance) for i in range(size)])


def per_device(positions, counts, kvec_x, kvec_y, kvec_z):
    groups = lax.axis_size("frames")
    bricks = lax.axis_size("bricks")
    frames_here, capacity = positions.shape[1], positions.shape[2]
    n_x, n_z = kvec_x.shape[0] // bricks, kvec_z.shape[0]
    rows = n_x * n_z
    share = kvec_y.shape[0] // groups
    block = frames_here * 2 * share
    vmem = pl.BlockSpec(memory_space=pltpu.VMEM)
    prods_shape = (frames_here, 2 * rows, 2 * KMAX)
    waves_shape = (n_x + n_z + 16, LANES)
    hbm = pl.BlockSpec(memory_space=pltpu.HBM)
    smem = pl.BlockSpec(memory_space=pltpu.SMEM)

    def density(shards, ids, sums, last):
        first = sums is None
        lanes = -(-len(ids) * capacity // (BIG * UNIT * LANES)) * BIG * UNIT * LANES
        args = [counts, kvec_x, kvec_z, shards] if first else [kvec_y] if last else []
        args = [pltpu.with_memory_space_constraint(arg, pltpu.HBM) for arg in args]
        scratch = [pltpu.SMEM(arg.shape, jnp.int32) for arg in args[:3]]
        scratch += [
            pltpu.VMEM((2 * rows, lanes), jnp.bfloat16),
            pltpu.VMEM((2 * KMAX, lanes), jnp.bfloat16),
            pltpu.VMEM((UNIT * 2 * (n_x + 8), LANES), jnp.float32),
            pltpu.SemaphoreType.DMA((4,)),
        ]
        if last:
            out_shape = [jax.ShapeDtypeStruct((block, rows), jnp.float32)] * groups
            scratch = [pltpu.VMEM(prods_shape, jnp.float32)] + scratch
        else:
            out_shape = [jax.ShapeDtypeStruct(prods_shape, jnp.float32)]
            if first:
                out_shape.append(jax.ShapeDtypeStruct(waves_shape, jnp.float32))
                out_shape.append(jax.ShapeDtypeStruct(counts.shape, jnp.int32))
                out_shape.append(jax.ShapeDtypeStruct(shards.shape, jnp.float32))
        atoms = frames_here * len(ids) * capacity
        return pl.pallas_call(
            functools.partial(density_kernel, ids, first, last, groups, n_x, n_z, share),
            out_shape=out_shape,
            in_specs=[hbm] * len(args) + ([] if first else [vmem] * 3 + [smem]),
            out_specs=[vmem, vmem, smem, vmem] if first else [vmem] * len(out_shape),
            scratch_shapes=scratch,
            cost_estimate=pl.CostEstimate(
                flops=atoms * rows * KMAX * 8, bytes_accessed=atoms * 12, transcendentals=0
            ),
            compiler_params=pltpu.CompilerParams(vmem_limit_bytes=48 << 20),
            name="density",
        )(*args, *([] if first else [shards, *sums]))

    held, fresh, ids = positions[None], positions[None], [0]
    new, sums, fixed = [0], None, None
    distance = bricks // 2
    while distance:
        got = swap(held, "bricks", bricks, distance)
        out = density(fresh, new, sums, False)
        if sums is None:
            fixed, held = out[1:3], out[3]
        got, prods = lax.optimization_barrier((got, out[0]))
        sums = (prods, *fixed)
        new = [i ^ distance for i in ids]
        ids, fresh = ids + new, got
        distance //= 2
        if distance:
            held = jnp.concatenate([held, got], axis=0)
    sends = density(fresh, new, sums, True)
    got = [sends[0]] + [swap(sends[d], "frames", groups, d) for d in range(1, groups)]

    chunk = min(8, share)
    frames_total = frames_here * groups
    return pl.pallas_call(
        functools.partial(
            spectrum_kernel, groups, share, chunk, n_x, n_z, frames_total, capacity * bricks
        ),
        out_shape=jax.ShapeDtypeStruct((n_x, share, n_z, NW), jnp.float32),
        in_specs=[vmem] * groups,
        out_specs=hbm,
        scratch_shapes=[
            pltpu.VMEM((n_x, share, n_z, NW), jnp.float32),
            pltpu.VMEM((groups * block, rows), jnp.float32),
            pltpu.VMEM((12 * frames_total, 4 * NW), jnp.bfloat16),
            pltpu.SemaphoreType.DMA((share // chunk,)),
        ],
        compiler_params=pltpu.CompilerParams(vmem_limit_bytes=16 << 20),
        name="spectrum",
    )(*got)


def solution(mesh):
    return jax.shard_map(
        per_device,
        mesh=mesh,
        in_specs=(P(None, "frames", "bricks"), P("frames", None), P(), P(), P()),
        out_specs=P("bricks", "frames", None, None),
        check_vma=False,
    )
```

profile of v0, /device:TPU:0, one launch (start us, length us, event | category | flops | bytes accessed | tf_op | source)
XLA Modules:
  0.0 34.5 jit_solution(11195150597086722342)
XLA Ops:
  0.0 4.0 %collective-permute-start = (f32[1,3,2,2048]{3,2,1,0:T(2,128)}, f32[1,3,2,2048]{3,2,1,0:T(2,128)S(1)}, u32[]{:S(2)}, u32[]{:S(2)}) collective-permute-start(f32[1,3,2,2048]{3,2,1,0:T(2,128)} %bitcast.1), channel_id=1, source_target_pairs={{0,4},{1,5},{2,6},{3,7},{4,0},{5,1},{6,2},{7,3},{8,12},{9,13},{10,... | collective-permute-start | bytes 147464 | tf_op jit(solution)/shard_map/ppermute | solution.py:290
  4.0 2.7 %density.4 = (f32[2,256,128]{2,1,0:T(8,128)S(1)}, f32[40,128]{1,0:T(8,128)S(1)}, s32[2,8]{1,0:T(2,128)S(1)}, f32[1,3,2,2048]{3,2,1,0:T(2,128)S(1)}) custom-call(s32[2,8]{1,0:T(2,128)} %refs_0_.2, s32[128]{0:T(128)} %refs_1_.1, s32[8]{0:T(128)} %refs_2_.1, f32[1,3,2,2048]{3,2,1,0:T(2,128)} %bitcast.2), custom_call_target="tpu_custom_call" | custom-call | flops 268435456 | bytes 49152 | tf_op jit(solution)/shard_map/density/pallas_call | solution.py:329
  6.7 0.1 collective-permute-done.refs_0_
  6.9 2.1 %collective-permute-start.1 = (f32[2,3,2,2048]{3,2,1,0:T(2,128)S(1)}, f32[2,3,2,2048]{3,2,1,0:T(2,128)S(1)}, u32[]{:S(2)}, u32[]{:S(2)}) collective-permute-start(f32[2,3,2,2048]{3,2,1,0:T(2,128)S(1)} %pad_maximum_fusion.1), channel_id=1, source_target_pairs={{0,2},{1,3},{2,0},{3,1},{4,6},{5,7},{6,4},{7,5},{8,10},{9,11},{10,... | collective-permute-start | bytes 294920 | tf_op jit(solution)/shard_map/ppermute | solution.py:290
  9.0 3.3 %density.5.refs_1_ = f32[2,256,128]{2,1,0:T(8,128)S(1)} custom-call(f32[1,3,2,2048]{3,2,1,0:T(2,128)S(1)} %collective-permute-done.refs_0_, f32[2,256,128]{2,1,0:T(8,128)S(1)} %get-tuple-element.22.refs_1_, f32[40,128]{1,0:T(8,128)S(1)} %get-tuple-element.23.refs_2_.refs_3_, s32[2,8]{1,0:T(2,128)S(1)} %get-tuple-element.24.refs_3_.refs_4_), custom_call_target="tpu_custom_call" | custom-call | flops 268435456 | bytes 49152 | tf_op jit(solution)/shard_map/density/pallas_call | solution.py:329
  12.3 0.0 collective-permute-done.1.refs_0_
  12.3 0.1 pad_maximum_fusion
  12.4 1.5 %collective-permute-start.2 = (f32[4,3,2,2048]{3,2,1,0:T(2,128)S(1)}, f32[4,3,2,2048]{3,2,1,0:T(2,128)S(1)}, u32[]{:S(2)}, u32[]{:S(2)}) collective-permute-start(f32[4,3,2,2048]{3,2,1,0:T(2,128)S(1)} %pad_maximum_fusion), channel_id=1, source_target_pairs={{0,1},{1,0},{2,3},{3,2},{4,5},{5,4},{6,7},{7,6},{8,9},{9,8},{10,11... | collective-permute-start | bytes 589832 | tf_op jit(solution)/shard_map/ppermute | solution.py:290
  13.9 2.9 %density.6.refs_2_ = f32[2,256,128]{2,1,0:T(8,128)S(1)} custom-call(f32[2,3,2,2048]{3,2,1,0:T(2,128)S(1)} %collective-permute-done.1.refs_0_, f32[2,256,128]{2,1,0:T(8,128)S(1)} %density.5.refs_1_, f32[40,128]{1,0:T(8,128)S(1)} %get-tuple-element.23.refs_2_.refs_3_, s32[2,8]{1,0:T(2,128)S(1)} %get-tuple-element.24.refs_3_.refs_4_), custom_call_target="tpu_custom_call" | custom-call | flops 536870912 | bytes 98304 | tf_op jit(solution)/shard_map/density/pallas_call | solution.py:329
  16.8 1.5 %collective-permute-done.2.refs_1_ = f32[4,3,2,2048]{3,2,1,0:T(2,128)S(1)} collective-permute-done((f32[4,3,2,2048]{3,2,1,0:T(2,128)S(1)}, f32[4,3,2,2048]{3,2,1,0:T(2,128)S(1)}, u32[]{:S(2)}, u32[]{:S(2)}) %collective-permute-start.2) | collective-permute-done | bytes 196640 | tf_op jit(solution)/shard_map/ppermute | solution.py:290
  18.3 6.4 %density.7 = (f32[128,128]{1,0:T(8,128)S(1)}, f32[128,128]{1,0:T(8,128)S(1)}, f32[128,128]{1,0:T(8,128)S(1)}, f32[128,128]{1,0:T(8,128)S(1)}) custom-call(s32[128]{0:T(128)} %refs_0_.3, f32[4,3,2,2048]{3,2,1,0:T(2,128)S(1)} %collective-permute-done.2.refs_1_, f32[2,256,128]{2,1,0:T(8,128)S(1)} %density.6.refs_2_, ...), custom_call_target="tpu_custom_call" | custom-call | flops 1073741824 | bytes 196608 | tf_op jit(solution)/shard_map/density/pallas_call | solution.py:329
  24.7 0.1 collective-permute-start.3
  24.7 3.5 %collective-permute-start.4 = (f32[128,128]{1,0:T(8,128)S(1)}, f32[128,128]{1,0:T(8,128)S(1)}, u32[]{:S(2)}, u32[]{:S(2)}) collective-permute-start(f32[128,128]{1,0:T(8,128)S(1)} %get-tuple-element.31), channel_id=1, source_target_pairs={{0,16},{8,24},{16,0},{24,8},{1,17},{9,25},{17,1},{25,9},{2,18},{10... | collective-permute-start | bytes 196616 | tf_op jit(solution)/shard_map/ppermute | solution.py:290
  28.2 0.0 collective-permute-start.5
  28.3 0.0 collective-permute-done.3.refs_1_
  28.3 2.3 %collective-permute-done.4.refs_2_ = f32[128,128]{1,0:T(8,128)S(1)} collective-permute-done((f32[128,128]{1,0:T(8,128)S(1)}, f32[128,128]{1,0:T(8,128)S(1)}, u32[]{:S(2)}, u32[]{:S(2)}) %collective-permute-start.4) | collective-permute-done | bytes 65568 | tf_op jit(solution)/shard_map/ppermute | solution.py:290
  30.6 2.0 %collective-permute-done.5.refs_3_ = f32[128,128]{1,0:T(8,128)S(1)} collective-permute-done((f32[128,128]{1,0:T(8,128)S(1)}, f32[128,128]{1,0:T(8,128)S(1)}, u32[]{:S(2)}, u32[]{:S(2)}) %collective-permute-start.5) | collective-permute-done | bytes 65568 | tf_op jit(solution)/shard_map/ppermute | solution.py:290
  32.6 1.7 %spectrum.1 = f32[16,32,8,128]{3,2,1,0:T(8,128)} custom-call(f32[128,128]{1,0:T(8,128)S(1)} %get-tuple-element.29.refs_0_, f32[128,128]{1,0:T(8,128)S(1)} %collective-permute-done.3.refs_1_, f32[128,128]{1,0:T(8,128)S(1)} %collective-permute-done.4.refs_2_, f32[128,128]{1,0:T(8,128)S(1)} %collective-permute-done.5.refs_3_), custom_call_target="tpu_custom_call" | custom-call | tf_op jit(solution)/shard_map/spectrum/pallas_call | solution.py:362
  (1 shorter events, 0.0 us)
Async XLA Ops:
  0.0 6.8 %collective-permute-start = (f32[1,3,2,2048]{3,2,1,0:T(2,128)}, f32[1,3,2,2048]{3,2,1,0:T(2,128)S(1)}, u32[]{:S(2)}, u32[]{:S(2)}) collective-permute-start(f32[1,3,2,2048]{3,2,1,0:T(2,128)} %bitcast.1), channel_id=1, source_target_pairs={{0,4},{1,5},{2,6},{3,7},{4,0},{5,1},{6,2},{7,3},{8,12},{9,13},{10,... | collective-permute-start | bytes 147464 | tf_op jit(solution)/shard_map/ppermute | solution.py:290
  6.9 5.4 %collective-permute-start.1 = (f32[2,3,2,2048]{3,2,1,0:T(2,128)S(1)}, f32[2,3,2,2048]{3,2,1,0:T(2,128)S(1)}, u32[]{:S(2)}, u32[]{:S(2)}) collective-permute-start(f32[2,3,2,2048]{3,2,1,0:T(2,128)S(1)} %pad_maximum_fusion.1), channel_id=1, source_target_pairs={{0,2},{1,3},{2,0},{3,1},{4,6},{5,7},{6,4},{7,5},{8,10},{9,11},{10,... | collective-permute-start | bytes 294920 | tf_op jit(solution)/shard_map/ppermute | solution.py:290
  12.4 5.9 %collective-permute-start.2 = (f32[4,3,2,2048]{3,2,1,0:T(2,128)S(1)}, f32[4,3,2,2048]{3,2,1,0:T(2,128)S(1)}, u32[]{:S(2)}, u32[]{:S(2)}) collective-permute-start(f32[4,3,2,2048]{3,2,1,0:T(2,128)S(1)} %pad_maximum_fusion), channel_id=1, source_target_pairs={{0,1},{1,0},{2,3},{3,2},{4,5},{5,4},{6,7},{7,6},{8,9},{9,8},{10,11... | collective-permute-start | bytes 589832 | tf_op jit(solution)/shard_map/ppermute | solution.py:290
  24.7 3.6 %collective-permute-start.3 = (f32[128,128]{1,0:T(8,128)S(1)}, f32[128,128]{1,0:T(8,128)S(1)}, u32[]{:S(2)}, u32[]{:S(2)}) collective-permute-start(f32[128,128]{1,0:T(8,128)S(1)} %get-tuple-element.30), channel_id=1, source_target_pairs={{0,8},{8,0},{16,24},{24,16},{1,9},{9,1},{17,25},{25,17},{2,10},{10... | collective-permute-start | bytes 196616 | tf_op jit(solution)/shard_map/ppermute | solution.py:290
  24.7 5.9 %collective-permute-start.4 = (f32[128,128]{1,0:T(8,128)S(1)}, f32[128,128]{1,0:T(8,128)S(1)}, u32[]{:S(2)}, u32[]{:S(2)}) collective-permute-start(f32[128,128]{1,0:T(8,128)S(1)} %get-tuple-element.31), channel_id=1, source_target_pairs={{0,16},{8,24},{16,0},{24,8},{1,17},{9,25},{17,1},{25,9},{2,18},{10... | collective-permute-start | bytes 196616 | tf_op jit(solution)/shard_map/ppermute | solution.py:290
  28.2 4.4 %collective-permute-start.5 = (f32[128,128]{1,0:T(8,128)S(1)}, f32[128,128]{1,0:T(8,128)S(1)}, u32[]{:S(2)}, u32[]{:S(2)}) collective-permute-start(f32[128,128]{1,0:T(8,128)S(1)} %get-tuple-element.32), channel_id=1, source_target_pairs={{0,24},{8,16},{16,8},{24,0},{1,25},{9,17},{17,9},{25,1},{2,26},{10... | collective-permute-start | bytes 196616 | tf_op jit(solution)/shard_map/ppermute | solution.py:290
where the time goes:
time: 34.3 us; the launch traced here: 34.5 us
  Pallas kernels  17 us (50%)
  starting transfers between devices  11.2 us (33%)
  waiting for transfers between devices  5.94 us (17%)
    pallas_call x4, Pallas kernels, density(): pl.pallas_call(functools.partial(density_kernel, ids, first, last, groups...  15.3 us
    ppermute x6, starting transfers between devices, swap(): return lax.ppermute(value, axis, [(i, i ^ distance) for i in range(size)])  11.2 us
    ppermute x6, waiting for transfers between devices, swap(): return lax.ppermute(value, axis, [(i, i ^ distance) for i in range(size)])  5.94 us
    pallas_call x1, Pallas kernels, per_device(): pl.pallas_call(functools.partial(spectrum_kernel, groups, share, chunk, n...  1.71 us
  transfers between devices with their start and end apart: 6, of which 4 were waited for; matrix products, arithmetic and copies ran while one was open for 0% of the time, Pallas kernels for 26%

commit v1 on v0

--- a/solution.py
+++ b/solution.py
@@ -41,26 +41,25 @@
     return 1.0 - half_s * half_s, half_s * half_c
 
 
-def density_kernel(ids, first, last, groups, n_x, n_z, share, *refs):
-    n_args = 4 if first else 1 if last else 0
+def density_kernel(unit, low, ids, first, last, groups, n_x, n_z, share, *refs):
+    n_args = 3 if first else 1 if last else 0
     args, refs = refs[:n_args], refs[n_args:]
     left_ref, right_ref, row_ref, arg_sem = refs[-4:]
     refs = refs[:-4]
+    pos_ref, refs = refs[0], refs[1:]
     if not first:
-        (pos_ref, prod_in, kb_ref, counts_ref), refs = refs[:4], refs[4:]
-    n_local = min(n_args, 3)
-    outs, local = refs[: len(refs) - n_local], refs[len(refs) - n_local :]
-    if first:
-        local = (*local, outs[3])
+        (prod_in, kb_ref, counts_ref), refs = refs[:3], refs[3:]
+    outs, local = refs[: len(refs) - n_args], refs[len(refs) - n_args :]
     copies = [
         pltpu.make_async_copy(args[i], local[i], arg_sem.at[i]) for i in range(n_args)
     ]
     for copy in copies:
         copy.start()
     if first:
-        counts_ref, pos_ref, kb_ref = local[0], local[3], outs[1]
+        counts_ref, kb_ref = local[0], outs[1]
     rows = n_x * n_z
-    n_shards, _, frames_here, capacity = pos_ref.shape
+    _, _, frames_here, capacity = pos_ref.shape
+    n_shards = len(ids)
     brick = lax.axis_index("bricks")
     lane = lax.broadcasted_iota(jnp.int32, (n_z, LANES), 1)
 
@@ -81,7 +80,6 @@
                 q = row - n_x - n_z
                 k = float(q + 1 if q < 8 else 8 * (q - 7))
             kb_ref[row : row + 1, :] = jnp.full((1, LANES), k, jnp.float32)
-        copies[3].wait()
 
     for frame in range(frames_here):
         counts = [counts_ref[frame, brick ^ d] for d in ids]
@@ -98,9 +96,9 @@
                 count = jnp.where(later, counts[s], count)
             offset = (item - start) * LANES
             where = pl.ds(pl.multiple_of(jnp.minimum(offset, capacity - LANES), LANES), LANES)
-            x = pos_ref[shard, 0, pl.ds(frame, 1), where]
-            y = pos_ref[shard, 1, pl.ds(frame, 1), where]
-            z = pos_ref[shard, 2, pl.ds(frame, 1), where]
+            x = pos_ref[low + shard, 0, pl.ds(frame, 1), where]
+            y = pos_ref[low + shard, 1, pl.ds(frame, 1), where]
+            z = pos_ref[low + shard, 2, pl.ds(frame, 1), where]
             cx, sx = cis(kb_ref[0:n_x, :] * x)
             cz, sz = cis(kb_ref[n_x : n_x + n_z, :] * z)
             cy, sy = cis(kb_ref[n_x + n_z : n_x + n_z + 16, :] * y)
@@ -139,19 +137,19 @@
                 right_ref[8 * q : 8 * q + 16, to] = jnp.concatenate(re[q : q + 2], axis=0).astype(jnp.bfloat16)
                 right_ref[KMAX + 8 * q : KMAX + 8 * q + 16, to] = jnp.concatenate(im[q : q + 2], axis=0).astype(jnp.bfloat16)
 
-        def build_unit(unit, carry, build=build):
-            for g in range(UNIT):
-                build(unit * UNIT + g, g)
+        def build_unit(at_unit, carry, build=build):
+            for g in range(unit):
+                build(at_unit * unit + g, g)
             return carry
 
-        units = (starts[-1] + UNIT - 1) // UNIT
+        units = (starts[-1] + unit - 1) // unit
         lax.fori_loop(0, units, build_unit, 0)
         prod_ref = outs[0].at[frame] if not last else outs[-1].at[frame]
         prod_ref[...] = jnp.zeros(prod_ref.shape, jnp.float32) if first else prod_in[frame]
 
         def multiply(width):
             def step(base):
-                where = pl.ds(pl.multiple_of(base, UNIT * LANES), width)
+                where = pl.ds(pl.multiple_of(base, unit * LANES), width)
                 prod_ref[...] += lax.dot_general(
                     left_ref[:, where],
                     right_ref[:, where],
@@ -161,11 +159,11 @@
 
             return step
 
-        wide = multiply(BIG * UNIT * LANES)
+        wide = multiply(BIG * unit * LANES)
         full = units // BIG
 
         def wide_step(i, carry, wide=wide):
-            wide(i * (BIG * UNIT * LANES))
+            wide(i * (BIG * unit * LANES))
             return carry
 
         lax.fori_loop(0, full, wide_step, 0)
@@ -173,7 +171,7 @@
 
             @pl.when(units - full * BIG == rest)
             def _(rest=rest, multiply=multiply, full=full):
-                multiply(rest * UNIT * LANES)(full * (BIG * UNIT * LANES))
+                multiply(rest * unit * LANES)(full * (BIG * unit * LANES))
 
     if last:
         copies[0].wait()
@@ -304,16 +302,17 @@
     hbm = pl.BlockSpec(memory_space=pltpu.HBM)
     smem = pl.BlockSpec(memory_space=pltpu.SMEM)
 
-    def density(shards, ids, sums, last):
+    def density(shards, low, ids, sums, last):
         first = sums is None
-        lanes = -(-len(ids) * capacity // (BIG * UNIT * LANES)) * BIG * UNIT * LANES
-        args = [counts, kvec_x, kvec_z, shards] if first else [kvec_y] if last else []
+        unit = UNIT if len(ids) > 1 else UNIT // 2
+        lanes = -(-len(ids) * capacity // (BIG * unit * LANES)) * BIG * unit * LANES
+        args = [counts, kvec_x, kvec_z] if first else [kvec_y] if last else []
         args = [pltpu.with_memory_space_constraint(arg, pltpu.HBM) for arg in args]
         scratch = [pltpu.SMEM(arg.shape, jnp.int32) for arg in args[:3]]
         scratch += [
             pltpu.VMEM((2 * rows, lanes), jnp.bfloat16),
             pltpu.VMEM((2 * KMAX, lanes), jnp.bfloat16),
-            pltpu.VMEM((UNIT * 2 * (n_x + 8), LANES), jnp.float32),
+            pltpu.VMEM((unit * 2 * (n_x + 8), LANES), jnp.float32),
             pltpu.SemaphoreType.DMA((4,)),
         ]
         if last:
@@ -324,37 +323,37 @@
             if first:
                 out_shape.append(jax.ShapeDtypeStruct(waves_shape, jnp.float32))
                 out_shape.append(jax.ShapeDtypeStruct(counts.shape, jnp.int32))
-                out_shape.append(jax.ShapeDtypeStruct(shards.shape, jnp.float32))
         atoms = frames_here * len(ids) * capacity
         return pl.pallas_call(
-            functools.partial(density_kernel, ids, first, last, groups, n_x, n_z, share),
+            functools.partial(density_kernel, unit, low, ids, first, last, groups, n_x, n_z, share),
             out_shape=out_shape,
-            in_specs=[hbm] * len(args) + ([] if first else [vmem] * 3 + [smem]),
-            out_specs=[vmem, vmem, smem, vmem] if first else [vmem] * len(out_shape),
+            in_specs=[hbm] * len(args) + [vmem] * (1 if first else 3) + ([] if first else [smem]),
+            out_specs=[vmem, vmem, smem] if first else [vmem] * len(out_shape),
             scratch_shapes=scratch,
             cost_estimate=pl.CostEstimate(
                 flops=atoms * rows * KMAX * 8, bytes_accessed=atoms * 12, transcendentals=0
             ),
             compiler_params=pltpu.CompilerParams(vmem_limit_bytes=48 << 20),
             name="density",
-        )(*args, *([] if first else [shards, *sums]))
-
-    held, fresh, ids = positions[None], positions[None], [0]
-    new, sums, fixed = [0], None, None
+        )(*args, shards, *([] if first else sums))
+
+    held, ids, done, sums = positions[None], [0], 0, None
     distance = bricks // 2
     while distance:
         got = swap(held, "bricks", bricks, distance)
-        out = density(fresh, new, sums, False)
-        if sums is None:
-            fixed, held = out[1:3], out[3]
-        got, prods = lax.optimization_barrier((got, out[0]))
-        sums = (prods, *fixed)
+        upto = len(ids) if distance == 1 else len(ids) // 2
+        if upto > done:
+            out = density(held, done, ids[done:upto], sums, False)
+            if sums is None:
+                fixed = out[1:]
+            got, prods = lax.optimization_barrier((got, out[0]))
+            sums, done = (prods, *fixed), upto
         new = [i ^ distance for i in ids]
-        ids, fresh = ids + new, got
+        ids = ids + new
         distance //= 2
         if distance:
             held = jnp.concatenate([held, got], axis=0)
-    sends = density(fresh, new, sums, True)
+    sends = density(got, 0, new, sums, True)
     got = [sends[0]] + [swap(sends[d], "frames", groups, d) for d in range(1, groups)]
 
     chunk = min(8, share)

time: 34.3 us -> 37.1 us (1.082)
  waiting for transfers between devices: 5.94 us -> 7.67 us
  other arithmetic: 0.14 us -> 1.74 us
  Pallas kernels: 17 us -> 16.1 us
    ppermute x6, waiting for transfers between devices: 5.94 us -> 7.67 us  [swap(): return lax.ppermute(value, axis, [(i, i ^ distance) for i in range(size)])]
    concatenate x2, other arithmetic: 0.14 us -> 1.74 us  [per_device(): held = jnp.concatenate([held, got], axis=0)]
    pallas_call x4 -> x3, Pallas kernels: 15.3 us -> 14.4 us  [density(): pl.pallas_call(functools.partial(density_kernel, unit, low, ids, first, l...]
  transfers between devices with their start and end apart: 6 -> 6, of which waited for: 4 -> 4; matrix products, arithmetic and copies ran while one was open for 0% -> 0% of each run, Pallas kernels for 26% -> 18%
where the time goes in v1:
time: 37.1 us; the launch traced here: 37 us
  Pallas kernels  16.1 us (43%)
  starting transfers between devices  11.3 us (30%)
  waiting for transfers between devices  7.67 us (21%)
  other arithmetic  1.74 us (5%)
    pallas_call x3, Pallas kernels, density(): pl.pallas_call(functools.partial(density_kernel, unit, low, ids, first, l...  14.4 us
    ppermute x6, starting transfers between devices, swap(): return lax.ppermute(value, axis, [(i, i ^ distance) for i in range(size)])  11.3 us
    ppermute x6, waiting for transfers between devices, swap(): return lax.ppermute(value, axis, [(i, i ^ distance) for i in range(size)])  7.67 us
    concatenate x2, other arithmetic, per_device(): held = jnp.concatenate([held, got], axis=0)  1.74 us
    pallas_call x1, Pallas kernels, per_device(): pl.pallas_call(functools.partial(spectrum_kernel, groups, share, chunk, n...  1.71 us
  transfers between devices with their start and end apart: 6, of which 4 were waited for; matrix products, arithmetic and copies ran while one was open for 0% of the time, Pallas kernels for 18%

profile of v1, /device:TPU:0, one launch (start us, length us, event | category | flops | bytes accessed | tf_op | source)
XLA Modules:
  0.0 37.0 jit_solution(893116471769632749)
XLA Ops:
  0.0 4.0 %collective-permute-start = (f32[1,3,2,2048]{3,2,1,0:T(2,128)}, f32[1,3,2,2048]{3,2,1,0:T(2,128)S(1)}, u32[]{:S(2)}, u32[]{:S(2)}) collective-permute-start(f32[1,3,2,2048]{3,2,1,0:T(2,128)} %bitcast.1), channel_id=1, source_target_pairs={{0,4},{1,5},{2,6},{3,7},{4,0},{5,1},{6,2},{7,3},{8,12},{9,13},{10,... | collective-permute-start | bytes 147464 | tf_op jit(solution)/shard_map/ppermute | solution.py:288
  4.0 2.8 %collective-permute-done = f32[1,3,2,2048]{3,2,1,0:T(2,128)S(1)} collective-permute-done((f32[1,3,2,2048]{3,2,1,0:T(2,128)}, f32[1,3,2,2048]{3,2,1,0:T(2,128)S(1)}, u32[]{:S(2)}, u32[]{:S(2)}) %collective-permute-start) | collective-permute-done | bytes 49184 | tf_op jit(solution)/shard_map/ppermute | solution.py:288
  6.8 0.8 %pad_maximum_fusion.1.refs_3_ = f32[2,3,2,2048]{3,2,1,0:T(2,128)S(1)} fusion(f32[1,3,2,2048]{3,2,1,0:T(2,128)S(1)} %collective-permute-done, f32[1,3,2,2048]{3,2,1,0:T(2,128)} %bitcast.2), kind=kLoop, calls=%fused_computation.1 | loop fusion | flops 24576 | bytes 196608 | tf_op jit(solution)/shard_map/concatenate | solution.py:355
  7.7 1.4 %collective-permute-start.1 = (f32[2,3,2,2048]{3,2,1,0:T(2,128)S(1)}, f32[2,3,2,2048]{3,2,1,0:T(2,128)S(1)}, u32[]{:S(2)}, u32[]{:S(2)}) collective-permute-start(f32[2,3,2,2048]{3,2,1,0:T(2,128)S(1)} %pad_maximum_fusion.1.refs_3_), channel_id=1, source_target_pairs={{0,2},{1,3},{2,0},{3,1},{4,6},{5,7},{6,4},{7,5},{8,10},{9,11},{10,... | collective-permute-start | bytes 294920 | tf_op jit(solution)/shard_map/ppermute | solution.py:288
  9.1 2.3 %density.3 = (f32[2,256,128]{2,1,0:T(8,128)S(1)}, f32[40,128]{1,0:T(8,128)S(1)}, s32[2,8]{1,0:T(2,128)S(1)}) custom-call(s32[2,8]{1,0:T(2,128)} %refs_0_.2, s32[128]{0:T(128)} %refs_1_.1, s32[8]{0:T(128)} %refs_2_.1, f32[2,3,2,2048]{3,2,1,0:T(2,128)S(1)} %pad_maximum_fusion.1.refs_3_), custom_call_target="tpu_custom_call" | custom-call | flops 268435456 | bytes 49152 | tf_op jit(solution)/shard_map/density/pallas_call | solution.py:327
  11.5 0.9 %collective-permute-done.1 = f32[2,3,2,2048]{3,2,1,0:T(2,128)S(1)} collective-permute-done((f32[2,3,2,2048]{3,2,1,0:T(2,128)S(1)}, f32[2,3,2,2048]{3,2,1,0:T(2,128)S(1)}, u32[]{:S(2)}, u32[]{:S(2)}) %collective-permute-start.1) | collective-permute-done | bytes 98336 | tf_op jit(solution)/shard_map/ppermute | solution.py:288
  12.4 0.9 %pad_maximum_fusion.refs_0_ = f32[4,3,2,2048]{3,2,1,0:T(2,128)S(1)} fusion(f32[2,3,2,2048]{3,2,1,0:T(2,128)S(1)} %collective-permute-done.1, f32[1,3,2,2048]{3,2,1,0:T(2,128)S(1)} %collective-permute-done, f32[1,3,2,2048]{3,2,1,0:T(2,128)} %bitcast.3), kind=kLoop, calls=%fused_computation | loop fusion | flops 98304 | bytes 393216 | tf_op jit(solution)/shard_map/concatenate | solution.py:355
  13.3 2.3 %collective-permute-start.2 = (f32[4,3,2,2048]{3,2,1,0:T(2,128)S(1)}, f32[4,3,2,2048]{3,2,1,0:T(2,128)S(1)}, u32[]{:S(2)}, u32[]{:S(2)}) collective-permute-start(f32[4,3,2,2048]{3,2,1,0:T(2,128)S(1)} %pad_maximum_fusion.refs_0_), channel_id=1, source_target_pairs={{0,1},{1,0},{2,3},{3,2},{4,5},{5,4},{6,7},{7,6},{8,9},{9,8},{10,11... | collective-permute-start | bytes 589832 | tf_op jit(solution)/shard_map/ppermute | solution.py:288
  15.6 4.2 %density.4.refs_2_ = f32[2,256,128]{2,1,0:T(8,128)S(1)} custom-call(f32[4,3,2,2048]{3,2,1,0:T(2,128)S(1)} %pad_maximum_fusion.refs_0_, f32[2,256,128]{2,1,0:T(8,128)S(1)} %get-tuple-element.18.refs_1_, f32[40,128]{1,0:T(8,128)S(1)} %get-tuple-element.19.refs_2_.refs_3_, s32[2,8]{1,0:T(2,128)S(1)} %get-tuple-element.20.refs_3_.refs_4_), custom_call_target="tpu_custom_call" | custom-call | flops 805306368 | bytes 147456 | tf_op jit(solution)/shard_map/density/pallas_call | solution.py:327
  19.9 0.0 collective-permute-done.2.refs_1_
  19.9 7.8 %density.5 = (f32[128,128]{1,0:T(8,128)S(1)}, f32[128,128]{1,0:T(8,128)S(1)}, f32[128,128]{1,0:T(8,128)S(1)}, f32[128,128]{1,0:T(8,128)S(1)}) custom-call(s32[128]{0:T(128)} %refs_0_.3, f32[4,3,2,2048]{3,2,1,0:T(2,128)S(1)} %collective-permute-done.2.refs_1_, f32[2,256,128]{2,1,0:T(8,128)S(1)} %density.4.refs_2_, ...), custom_call_target="tpu_custom_call" | custom-call | flops 1073741824 | bytes 196608 | tf_op jit(solution)/shard_map/density/pallas_call | solution.py:327
  27.7 0.1 collective-permute-start.3
  27.8 3.3 %collective-permute-start.4 = (f32[128,128]{1,0:T(8,128)S(1)}, f32[128,128]{1,0:T(8,128)S(1)}, u32[]{:S(2)}, u32[]{:S(2)}) collective-permute-start(f32[128,128]{1,0:T(8,128)S(1)} %get-tuple-element.25), channel_id=1, source_target_pairs={{0,16},{8,24},{16,0},{24,8},{1,17},{9,25},{17,1},{25,9},{2,18},{10... | collective-permute-start | bytes 196616 | tf_op jit(solution)/shard_map/ppermute | solution.py:288
  31.1 0.1 collective-permute-start.5
  31.2 0.0 collective-permute-done.3.refs_1_
  31.2 2.6 %collective-permute-done.4.refs_2_ = f32[128,128]{1,0:T(8,128)S(1)} collective-permute-done((f32[128,128]{1,0:T(8,128)S(1)}, f32[128,128]{1,0:T(8,128)S(1)}, u32[]{:S(2)}, u32[]{:S(2)}) %collective-permute-start.4) | collective-permute-done | bytes 65568 | tf_op jit(solution)/shard_map/ppermute | solution.py:288
  33.8 1.4 %collective-permute-done.5.refs_3_ = f32[128,128]{1,0:T(8,128)S(1)} collective-permute-done((f32[128,128]{1,0:T(8,128)S(1)}, f32[128,128]{1,0:T(8,128)S(1)}, u32[]{:S(2)}, u32[]{:S(2)}) %collective-permute-start.5) | collective-permute-done | bytes 65568 | tf_op jit(solution)/shard_map/ppermute | solution.py:288
  35.1 1.7 %spectrum.1 = f32[16,32,8,128]{3,2,1,0:T(8,128)} custom-call(f32[128,128]{1,0:T(8,128)S(1)} %get-tuple-element.23.refs_0_, f32[128,128]{1,0:T(8,128)S(1)} %collective-permute-done.3.refs_1_, f32[128,128]{1,0:T(8,128)S(1)} %collective-permute-done.4.refs_2_, f32[128,128]{1,0:T(8,128)S(1)} %collective-permute-done.5.refs_3_), custom_call_target="tpu_custom_call" | custom-call | tf_op jit(solution)/shard_map/spectrum/pallas_call | solution.py:361
Async XLA Ops:
  0.0 6.8 %collective-permute-start = (f32[1,3,2,2048]{3,2,1,0:T(2,128)}, f32[1,3,2,2048]{3,2,1,0:T(2,128)S(1)}, u32[]{:S(2)}, u32[]{:S(2)}) collective-permute-start(f32[1,3,2,2048]{3,2,1,0:T(2,128)} %bitcast.1), channel_id=1, source_target_pairs={{0,4},{1,5},{2,6},{3,7},{4,0},{5,1},{6,2},{7,3},{8,12},{9,13},{10,... | collective-permute-start | bytes 147464 | tf_op jit(solution)/shard_map/ppermute | solution.py:288
  7.7 4.7 %collective-permute-start.1 = (f32[2,3,2,2048]{3,2,1,0:T(2,128)S(1)}, f32[2,3,2,2048]{3,2,1,0:T(2,128)S(1)}, u32[]{:S(2)}, u32[]{:S(2)}) collective-permute-start(f32[2,3,2,2048]{3,2,1,0:T(2,128)S(1)} %pad_maximum_fusion.1.refs_3_), channel_id=1, source_target_pairs={{0,2},{1,3},{2,0},{3,1},{4,6},{5,7},{6,4},{7,5},{8,10},{9,11},{10,... | collective-permute-start | bytes 294920 | tf_op jit(solution)/shard_map/ppermute | solution.py:288
  13.3 6.6 %collective-permute-start.2 = (f32[4,3,2,2048]{3,2,1,0:T(2,128)S(1)}, f32[4,3,2,2048]{3,2,1,0:T(2,128)S(1)}, u32[]{:S(2)}, u32[]{:S(2)}) collective-permute-start(f32[4,3,2,2048]{3,2,1,0:T(2,128)S(1)} %pad_maximum_fusion.refs_0_), channel_id=1, source_target_pairs={{0,1},{1,0},{2,3},{3,2},{4,5},{5,4},{6,7},{7,6},{8,9},{9,8},{10,11... | collective-permute-start | bytes 589832 | tf_op jit(solution)/shard_map/ppermute | solution.py:288
  27.7 3.5 %collective-permute-start.3 = (f32[128,128]{1,0:T(8,128)S(1)}, f32[128,128]{1,0:T(8,128)S(1)}, u32[]{:S(2)}, u32[]{:S(2)}) collective-permute-start(f32[128,128]{1,0:T(8,128)S(1)} %get-tuple-element.24), channel_id=1, source_target_pairs={{0,8},{8,0},{16,24},{24,16},{1,9},{9,1},{17,25},{25,17},{2,10},{10... | collective-permute-start | bytes 196616 | tf_op jit(solution)/shard_map/ppermute | solution.py:288
  27.8 6.0 %collective-permute-start.4 = (f32[128,128]{1,0:T(8,128)S(1)}, f32[128,128]{1,0:T(8,128)S(1)}, u32[]{:S(2)}, u32[]{:S(2)}) collective-permute-start(f32[128,128]{1,0:T(8,128)S(1)} %get-tuple-element.25), channel_id=1, source_target_pairs={{0,16},{8,24},{16,0},{24,8},{1,17},{9,25},{17,1},{25,9},{2,18},{10... | collective-permute-start | bytes 196616 | tf_op jit(solution)/shard_map/ppermute | solution.py:288
  31.1 4.0 %collective-permute-start.5 = (f32[128,128]{1,0:T(8,128)S(1)}, f32[128,128]{1,0:T(8,128)S(1)}, u32[]{:S(2)}, u32[]{:S(2)}) collective-permute-start(f32[128,128]{1,0:T(8,128)S(1)} %get-tuple-element.26), channel_id=1, source_target_pairs={{0,24},{8,16},{16,8},{24,0},{1,25},{9,17},{17,9},{25,1},{2,26},{10... | collective-permute-start | bytes 196616 | tf_op jit(solution)/shard_map/ppermute | solution.py:288

commit v2 on v0

--- a/solution.py
+++ b/solution.py
@@ -41,7 +41,7 @@
     return 1.0 - half_s * half_s, half_s * half_c
 
 
-def density_kernel(ids, first, last, groups, n_x, n_z, share, *refs):
+def density_kernel(unit, ids, first, last, groups, n_x, n_z, share, *refs):
     n_args = 4 if first else 1 if last else 0
     args, refs = refs[:n_args], refs[n_args:]
     left_ref, right_ref, row_ref, arg_sem = refs[-4:]
@@ -139,19 +139,19 @@
                 right_ref[8 * q : 8 * q + 16, to] = jnp.concatenate(re[q : q + 2], axis=0).astype(jnp.bfloat16)
                 right_ref[KMAX + 8 * q : KMAX + 8 * q + 16, to] = jnp.concatenate(im[q : q + 2], axis=0).astype(jnp.bfloat16)
 
-        def build_unit(unit, carry, build=build):
-            for g in range(UNIT):
-                build(unit * UNIT + g, g)
+        def build_unit(at_unit, carry, build=build):
+            for g in range(unit):
+                build(at_unit * unit + g, g)
             return carry
 
-        units = (starts[-1] + UNIT - 1) // UNIT
+        units = (starts[-1] + unit - 1) // unit
         lax.fori_loop(0, units, build_unit, 0)
         prod_ref = outs[0].at[frame] if not last else outs[-1].at[frame]
         prod_ref[...] = jnp.zeros(prod_ref.shape, jnp.float32) if first else prod_in[frame]
 
         def multiply(width):
             def step(base):
-                where = pl.ds(pl.multiple_of(base, UNIT * LANES), width)
+                where = pl.ds(pl.multiple_of(base, unit * LANES), width)
                 prod_ref[...] += lax.dot_general(
                     left_ref[:, where],
                     right_ref[:, where],
@@ -161,11 +161,11 @@
 
             return step
 
-        wide = multiply(BIG * UNIT * LANES)
+        wide = multiply(BIG * unit * LANES)
         full = units // BIG
 
         def wide_step(i, carry, wide=wide):
-            wide(i * (BIG * UNIT * LANES))
+            wide(i * (BIG * unit * LANES))
             return carry
 
         lax.fori_loop(0, full, wide_step, 0)
@@ -173,7 +173,7 @@
 
             @pl.when(units - full * BIG == rest)
             def _(rest=rest, multiply=multiply, full=full):
-                multiply(rest * UNIT * LANES)(full * (BIG * UNIT * LANES))
+                multiply(rest * unit * LANES)(full * (BIG * unit * LANES))
 
     if last:
         copies[0].wait()
@@ -306,14 +306,15 @@
 
     def density(shards, ids, sums, last):
         first = sums is None
-        lanes = -(-len(ids) * capacity // (BIG * UNIT * LANES)) * BIG * UNIT * LANES
+        unit = UNIT if len(ids) > 1 else UNIT // 2
+        lanes = -(-len(ids) * capacity // (BIG * unit * LANES)) * BIG * unit * LANES
         args = [counts, kvec_x, kvec_z, shards] if first else [kvec_y] if last else []
         args = [pltpu.with_memory_space_constraint(arg, pltpu.HBM) for arg in args]
         scratch = [pltpu.SMEM(arg.shape, jnp.int32) for arg in args[:3]]
         scratch += [
             pltpu.VMEM((2 * rows, lanes), jnp.bfloat16),
             pltpu.VMEM((2 * KMAX, lanes), jnp.bfloat16),
-            pltpu.VMEM((UNIT * 2 * (n_x + 8), LANES), jnp.float32),
+            pltpu.VMEM((unit * 2 * (n_x + 8), LANES), jnp.float32),
             pltpu.SemaphoreType.DMA((4,)),
         ]
         if last:
@@ -327,7 +328,7 @@
                 out_shape.append(jax.ShapeDtypeStruct(shards.shape, jnp.float32))
         atoms = frames_here * len(ids) * capacity
         return pl.pallas_call(
-            functools.partial(density_kernel, ids, first, last, groups, n_x, n_z, share),
+            functools.partial(density_kernel, unit, ids, first, last, groups, n_x, n_z, share),
             out_shape=out_shape,
             in_specs=[hbm] * len(args) + ([] if first else [vmem] * 3 + [smem]),
             out_specs=[vmem, vmem, smem, vmem] if first else [vmem] * len(out_shape),

time: 34.3 us -> 33.3 us (0.971); the launches traced: 34.5 us -> 33.9 us
  waiting for transfers between devices: 5.94 us -> 4.91 us
  Pallas kernels: 17 us -> 17.9 us
  starting transfers between devices: 11.2 us -> 10.7 us
    ppermute x6, waiting for transfers between devices: 5.94 us -> 4.91 us  [swap(): return lax.ppermute(value, axis, [(i, i ^ distance) for i in range(size)])]
    pallas_call x4, Pallas kernels: 15.3 us -> 16.2 us  [density(): pl.pallas_call(functools.partial(density_kernel, unit, ids, first, last,...]
    ppermute x6, starting transfers between devices: 11.2 us -> 10.7 us  [swap(): return lax.ppermute(value, axis, [(i, i ^ distance) for i in range(size)])]
  transfers between devices with their start and end apart: 6 -> 6, of which waited for: 4 -> 3; matrix products, arithmetic and copies ran while one was open for 0% -> 0% of each run, Pallas kernels for 26% -> 30%
where the time goes in v2:
time: 33.3 us; the launch traced here: 33.9 us
  Pallas kernels  17.9 us (54%)
  starting transfers between devices  10.7 us (32%)
  waiting for transfers between devices  4.91 us (15%)
    pallas_call x4, Pallas kernels, density(): pl.pallas_call(functools.partial(density_kernel, unit, ids, first, last,...  16.2 us
    ppermute x6, starting transfers between devices, swap(): return lax.ppermute(value, axis, [(i, i ^ distance) for i in range(size)])  10.7 us
    ppermute x6, waiting for transfers between devices, swap(): return lax.ppermute(value, axis, [(i, i ^ distance) for i in range(size)])  4.91 us
    pallas_call x1, Pallas kernels, per_device(): pl.pallas_call(functools.partial(spectrum_kernel, groups, share, chunk, n...  1.71 us
  transfers between devices with their start and end apart: 6, of which 3 were waited for; matrix products, arithmetic and copies ran while one was open for 0% of the time, Pallas kernels for 30%

profile of v2, /device:TPU:0, one launch (start us, length us, event | category | flops | bytes accessed | tf_op | source)
XLA Modules:
  0.0 33.9 jit_solution(8903879339178300762)
XLA Ops:
  0.0 4.0 %collective-permute-start = (f32[1,3,2,2048]{3,2,1,0:T(2,128)}, f32[1,3,2,2048]{3,2,1,0:T(2,128)S(1)}, u32[]{:S(2)}, u32[]{:S(2)}) collective-permute-start(f32[1,3,2,2048]{3,2,1,0:T(2,128)} %bitcast.1), channel_id=1, source_target_pairs={{0,4},{1,5},{2,6},{3,7},{4,0},{5,1},{6,2},{7,3},{8,12},{9,13},{10,... | collective-permute-start | bytes 147464 | tf_op jit(solution)/shard_map/ppermute | solution.py:290
  4.0 2.8 %density.4 = (f32[2,256,128]{2,1,0:T(8,128)S(1)}, f32[40,128]{1,0:T(8,128)S(1)}, s32[2,8]{1,0:T(2,128)S(1)}, f32[1,3,2,2048]{3,2,1,0:T(2,128)S(1)}) custom-call(s32[2,8]{1,0:T(2,128)} %refs_0_.2, s32[128]{0:T(128)} %refs_1_.1, s32[8]{0:T(128)} %refs_2_.1, f32[1,3,2,2048]{3,2,1,0:T(2,128)} %bitcast.2), custom_call_target="tpu_custom_call" | custom-call | flops 268435456 | bytes 49152 | tf_op jit(solution)/shard_map/density/pallas_call | solution.py:330
  6.9 0.0 collective-permute-done.refs_0_
  6.9 2.8 %collective-permute-start.1 = (f32[2,3,2,2048]{3,2,1,0:T(2,128)S(1)}, f32[2,3,2,2048]{3,2,1,0:T(2,128)S(1)}, u32[]{:S(2)}, u32[]{:S(2)}) collective-permute-start(f32[2,3,2,2048]{3,2,1,0:T(2,128)S(1)} %pad_maximum_fusion.1), channel_id=1, source_target_pairs={{0,2},{1,3},{2,0},{3,1},{4,6},{5,7},{6,4},{7,5},{8,10},{9,11},{10,... | collective-permute-start | bytes 294920 | tf_op jit(solution)/shard_map/ppermute | solution.py:290
  9.7 2.3 %density.5.refs_1_ = f32[2,256,128]{2,1,0:T(8,128)S(1)} custom-call(f32[1,3,2,2048]{3,2,1,0:T(2,128)S(1)} %collective-permute-done.refs_0_, f32[2,256,128]{2,1,0:T(8,128)S(1)} %get-tuple-element.22.refs_1_, f32[40,128]{1,0:T(8,128)S(1)} %get-tuple-element.23.refs_2_.refs_3_, s32[2,8]{1,0:T(2,128)S(1)} %get-tuple-element.24.refs_3_.refs_4_), custom_call_target="tpu_custom_call" | custom-call | flops 268435456 | bytes 49152 | tf_op jit(solution)/shard_map/density/pallas_call | solution.py:330
  12.0 0.5 %collective-permute-done.1.refs_0_ = f32[2,3,2,2048]{3,2,1,0:T(2,128)S(1)} collective-permute-done((f32[2,3,2,2048]{3,2,1,0:T(2,128)S(1)}, f32[2,3,2,2048]{3,2,1,0:T(2,128)S(1)}, u32[]{:S(2)}, u32[]{:S(2)}) %collective-permute-start.1) | collective-permute-done | bytes 98336 | tf_op jit(solution)/shard_map/ppermute | solution.py:290
  12.5 0.1 pad_maximum_fusion
  12.6 1.2 %collective-permute-start.2 = (f32[4,3,2,2048]{3,2,1,0:T(2,128)S(1)}, f32[4,3,2,2048]{3,2,1,0:T(2,128)S(1)}, u32[]{:S(2)}, u32[]{:S(2)}) collective-permute-start(f32[4,3,2,2048]{3,2,1,0:T(2,128)S(1)} %pad_maximum_fusion), channel_id=1, source_target_pairs={{0,1},{1,0},{2,3},{3,2},{4,5},{5,4},{6,7},{7,6},{8,9},{9,8},{10,11... | collective-permute-start | bytes 589832 | tf_op jit(solution)/shard_map/ppermute | solution.py:290
  13.8 4.9 %density.6.refs_2_ = f32[2,256,128]{2,1,0:T(8,128)S(1)} custom-call(f32[2,3,2,2048]{3,2,1,0:T(2,128)S(1)} %collective-permute-done.1.refs_0_, f32[2,256,128]{2,1,0:T(8,128)S(1)} %density.5.refs_1_, f32[40,128]{1,0:T(8,128)S(1)} %get-tuple-element.23.refs_2_.refs_3_, s32[2,8]{1,0:T(2,128)S(1)} %get-tuple-element.24.refs_3_.refs_4_), custom_call_target="tpu_custom_call" | custom-call | flops 536870912 | bytes 98304 | tf_op jit(solution)/shard_map/density/pallas_call | solution.py:330
  18.8 0.0 collective-permute-done.2.refs_1_
  18.8 6.2 %density.7 = (f32[128,128]{1,0:T(8,128)S(1)}, f32[128,128]{1,0:T(8,128)S(1)}, f32[128,128]{1,0:T(8,128)S(1)}, f32[128,128]{1,0:T(8,128)S(1)}) custom-call(s32[128]{0:T(128)} %refs_0_.3, f32[4,3,2,2048]{3,2,1,0:T(2,128)S(1)} %collective-permute-done.2.refs_1_, f32[2,256,128]{2,1,0:T(8,128)S(1)} %density.6.refs_2_, ...), custom_call_target="tpu_custom_call" | custom-call | flops 1073741824 | bytes 196608 | tf_op jit(solution)/shard_map/density/pallas_call | solution.py:330
  25.0 0.1 collective-permute-start.3
  25.0 2.6 %collective-permute-start.4 = (f32[128,128]{1,0:T(8,128)S(1)}, f32[128,128]{1,0:T(8,128)S(1)}, u32[]{:S(2)}, u32[]{:S(2)}) collective-permute-start(f32[128,128]{1,0:T(8,128)S(1)} %get-tuple-element.31), channel_id=1, source_target_pairs={{0,16},{8,24},{16,0},{24,8},{1,17},{9,25},{17,1},{25,9},{2,18},{10... | collective-permute-start | bytes 196616 | tf_op jit(solution)/shard_map/ppermute | solution.py:290
  27.6 0.0 collective-permute-start.5
  27.6 0.0 collective-permute-done.3.refs_1_
  27.6 2.3 %collective-permute-done.4.refs_2_ = f32[128,128]{1,0:T(8,128)S(1)} collective-permute-done((f32[128,128]{1,0:T(8,128)S(1)}, f32[128,128]{1,0:T(8,128)S(1)}, u32[]{:S(2)}, u32[]{:S(2)}) %collective-permute-start.4) | collective-permute-done | bytes 65568 | tf_op jit(solution)/shard_map/ppermute | solution.py:290
  30.0 2.0 %collective-permute-done.5.refs_3_ = f32[128,128]{1,0:T(8,128)S(1)} collective-permute-done((f32[128,128]{1,0:T(8,128)S(1)}, f32[128,128]{1,0:T(8,128)S(1)}, u32[]{:S(2)}, u32[]{:S(2)}) %collective-permute-start.5) | collective-permute-done | bytes 65568 | tf_op jit(solution)/shard_map/ppermute | solution.py:290
  32.0 1.7 %spectrum.1 = f32[16,32,8,128]{3,2,1,0:T(8,128)} custom-call(f32[128,128]{1,0:T(8,128)S(1)} %get-tuple-element.29.refs_0_, f32[128,128]{1,0:T(8,128)S(1)} %collective-permute-done.3.refs_1_, f32[128,128]{1,0:T(8,128)S(1)} %collective-permute-done.4.refs_2_, f32[128,128]{1,0:T(8,128)S(1)} %collective-permute-done.5.refs_3_), custom_call_target="tpu_custom_call" | custom-call | tf_op jit(solution)/shard_map/spectrum/pallas_call | solution.py:363
  (1 shorter events, 0.0 us)
Async XLA Ops:
  0.0 6.9 %collective-permute-start = (f32[1,3,2,2048]{3,2,1,0:T(2,128)}, f32[1,3,2,2048]{3,2,1,0:T(2,128)S(1)}, u32[]{:S(2)}, u32[]{:S(2)}) collective-permute-start(f32[1,3,2,2048]{3,2,1,0:T(2,128)} %bitcast.1), channel_id=1, source_target_pairs={{0,4},{1,5},{2,6},{3,7},{4,0},{5,1},{6,2},{7,3},{8,12},{9,13},{10,... | collective-permute-start | bytes 147464 | tf_op jit(solution)/shard_map/ppermute | solution.py:290
  6.9 5.6 %collective-permute-start.1 = (f32[2,3,2,2048]{3,2,1,0:T(2,128)S(1)}, f32[2,3,2,2048]{3,2,1,0:T(2,128)S(1)}, u32[]{:S(2)}, u32[]{:S(2)}) collective-permute-start(f32[2,3,2,2048]{3,2,1,0:T(2,128)S(1)} %pad_maximum_fusion.1), channel_id=1, source_target_pairs={{0,2},{1,3},{2,0},{3,1},{4,6},{5,7},{6,4},{7,5},{8,10},{9,11},{10,... | collective-permute-start | bytes 294920 | tf_op jit(solution)/shard_map/ppermute | solution.py:290
  12.6 6.2 %collective-permute-start.2 = (f32[4,3,2,2048]{3,2,1,0:T(2,128)S(1)}, f32[4,3,2,2048]{3,2,1,0:T(2,128)S(1)}, u32[]{:S(2)}, u32[]{:S(2)}) collective-permute-start(f32[4,3,2,2048]{3,2,1,0:T(2,128)S(1)} %pad_maximum_fusion), channel_id=1, source_target_pairs={{0,1},{1,0},{2,3},{3,2},{4,5},{5,4},{6,7},{7,6},{8,9},{9,8},{10,11... | collective-permute-start | bytes 589832 | tf_op jit(solution)/shard_map/ppermute | solution.py:290
  25.0 2.7 %collective-permute-start.3 = (f32[128,128]{1,0:T(8,128)S(1)}, f32[128,128]{1,0:T(8,128)S(1)}, u32[]{:S(2)}, u32[]{:S(2)}) collective-permute-start(f32[128,128]{1,0:T(8,128)S(1)} %get-tuple-element.30), channel_id=1, source_target_pairs={{0,8},{8,0},{16,24},{24,16},{1,9},{9,1},{17,25},{25,17},{2,10},{10... | collective-permute-start | bytes 196616 | tf_op jit(solution)/shard_map/ppermute | solution.py:290
  25.0 4.9 %collective-permute-start.4 = (f32[128,128]{1,0:T(8,128)S(1)}, f32[128,128]{1,0:T(8,128)S(1)}, u32[]{:S(2)}, u32[]{:S(2)}) collective-permute-start(f32[128,128]{1,0:T(8,128)S(1)} %get-tuple-element.31), channel_id=1, source_target_pairs={{0,16},{8,24},{16,0},{24,8},{1,17},{9,25},{17,1},{25,9},{2,18},{10... | collective-permute-start | bytes 196616 | tf_op jit(solution)/shard_map/ppermute | solution.py:290
  27.6 4.4 %collective-permute-start.5 = (f32[128,128]{1,0:T(8,128)S(1)}, f32[128,128]{1,0:T(8,128)S(1)}, u32[]{:S(2)}, u32[]{:S(2)}) collective-permute-start(f32[128,128]{1,0:T(8,128)S(1)} %get-tuple-element.32), channel_id=1, source_target_pairs={{0,24},{8,16},{16,8},{24,0},{1,25},{9,17},{17,9},{25,1},{2,26},{10... | collective-permute-start | bytes 196616 | tf_op jit(solution)/shard_map/ppermute | solution.py:290

commit v3 on v2

--- a/solution.py
+++ b/solution.py
@@ -306,7 +306,7 @@
 
     def density(shards, ids, sums, last):
         first = sums is None
-        unit = UNIT if len(ids) > 1 else UNIT // 2
+        unit = UNIT if len(ids) > 2 else UNIT // 2
         lanes = -(-len(ids) * capacity // (BIG * unit * LANES)) * BIG * unit * LANES
         args = [counts, kvec_x, kvec_z, shards] if first else [kvec_y] if last else []
         args = [pltpu.with_memory_space_constraint(arg, pltpu.HBM) for arg in args]
@@ -356,7 +356,8 @@
         if distance:
             held = jnp.concatenate([held, got], axis=0)
     sends = density(fresh, new, sums, True)
-    got = [sends[0]] + [swap(sends[d], "frames", groups, d) for d in range(1, groups)]
+    far = [swap(sends[d], "frames", groups, d) for d in range(groups - 1, 0, -1)]
+    got = [sends[0]] + far[::-1]
 
     chunk = min(8, share)
     frames_total = frames_here * groups

time: 33.3 us -> 34.6 us (1.039)
  Pallas kernels: 17.9 us -> 20.9 us
  starting transfers between devices: 10.7 us -> 9.27 us
  waiting for transfers between devices: 4.91 us -> 4.34 us
    pallas_call x4, Pallas kernels: 16.2 us -> 19.2 us  [density(): pl.pallas_call(functools.partial(density_kernel, unit, ids, first, last,...]
    ppermute x6, starting transfers between devices: 10.7 us -> 9.27 us  [swap(): return lax.ppermute(value, axis, [(i, i ^ distance) for i in range(size)])]
    ppermute x6, waiting for transfers between devices: 4.91 us -> 4.34 us  [swap(): return lax.ppermute(value, axis, [(i, i ^ distance) for i in range(size)])]
  transfers between devices with their start and end apart: 6 -> 6, of which waited for: 3 -> 4; matrix products, arithmetic and copies ran while one was open for 0% -> 0% of each run, Pallas kernels for 30% -> 29%
where the time goes in v3:
time: 34.6 us; the launch traced here: 34.9 us
  Pallas kernels  20.9 us (60%)
  starting transfers between devices  9.27 us (27%)
  waiting for transfers between devices  4.34 us (13%)
    pallas_call x4, Pallas kernels, density(): pl.pallas_call(functools.partial(density_kernel, unit, ids, first, last,...  19.2 us
    ppermute x6, starting transfers between devices, swap(): return lax.ppermute(value, axis, [(i, i ^ distance) for i in range(size)])  9.27 us
    ppermute x6, waiting for transfers between devices, swap(): return lax.ppermute(value, axis, [(i, i ^ distance) for i in range(size)])  4.34 us
    pallas_call x1, Pallas kernels, per_device(): pl.pallas_call(functools.partial(spectrum_kernel, groups, share, chunk, n...  1.71 us
  transfers between devices with their start and end apart: 6, of which 4 were waited for; matrix products, arithmetic and copies ran while one was open for 0% of the time, Pallas kernels for 29%

profile of v3, /device:TPU:0, one launch (start us, length us, event | category | flops | bytes accessed | tf_op | source)
XLA Modules:
  0.0 34.9 jit_solution(16799580770769021150)
XLA Ops:
  0.0 4.0 %collective-permute-start = (f32[1,3,2,2048]{3,2,1,0:T(2,128)}, f32[1,3,2,2048]{3,2,1,0:T(2,128)S(1)}, u32[]{:S(2)}, u32[]{:S(2)}) collective-permute-start(f32[1,3,2,2048]{3,2,1,0:T(2,128)} %bitcast.1), channel_id=1, source_target_pairs={{0,4},{1,5},{2,6},{3,7},{4,0},{5,1},{6,2},{7,3},{8,12},{9,13},{10,... | collective-permute-start | bytes 147464 | tf_op jit(solution)/shard_map/ppermute | solution.py:290
  4.0 3.4 %density.4 = (f32[2,256,128]{2,1,0:T(8,128)S(1)}, f32[40,128]{1,0:T(8,128)S(1)}, s32[2,8]{1,0:T(2,128)S(1)}, f32[1,3,2,2048]{3,2,1,0:T(2,128)S(1)}) custom-call(s32[2,8]{1,0:T(2,128)} %refs_0_.2, s32[128]{0:T(128)} %refs_1_.1, s32[8]{0:T(128)} %refs_2_.1, f32[1,3,2,2048]{3,2,1,0:T(2,128)} %bitcast.2), custom_call_target="tpu_custom_call" | custom-call | flops 268435456 | bytes 49152 | tf_op jit(solution)/shard_map/density/pallas_call | solution.py:330
  7.4 0.0 collective-permute-done.refs_0_
  7.5 1.2 %collective-permute-start.1 = (f32[2,3,2,2048]{3,2,1,0:T(2,128)S(1)}, f32[2,3,2,2048]{3,2,1,0:T(2,128)S(1)}, u32[]{:S(2)}, u32[]{:S(2)}) collective-permute-start(f32[2,3,2,2048]{3,2,1,0:T(2,128)S(1)} %pad_maximum_fusion.1), channel_id=1, source_target_pairs={{0,2},{1,3},{2,0},{3,1},{4,6},{5,7},{6,4},{7,5},{8,10},{9,11},{10,... | collective-permute-start | bytes 294920 | tf_op jit(solution)/shard_map/ppermute | solution.py:290
  8.7 3.1 %density.5.refs_1_ = f32[2,256,128]{2,1,0:T(8,128)S(1)} custom-call(f32[1,3,2,2048]{3,2,1,0:T(2,128)S(1)} %collective-permute-done.refs_0_, f32[2,256,128]{2,1,0:T(8,128)S(1)} %get-tuple-element.22.refs_1_, f32[40,128]{1,0:T(8,128)S(1)} %get-tuple-element.23.refs_2_.refs_3_, s32[2,8]{1,0:T(2,128)S(1)} %get-tuple-element.24.refs_3_.refs_4_), custom_call_target="tpu_custom_call" | custom-call | flops 268435456 | bytes 49152 | tf_op jit(solution)/shard_map/density/pallas_call | solution.py:330
  11.8 0.4 %collective-permute-done.1.refs_0_ = f32[2,3,2,2048]{3,2,1,0:T(2,128)S(1)} collective-permute-done((f32[2,3,2,2048]{3,2,1,0:T(2,128)S(1)}, f32[2,3,2,2048]{3,2,1,0:T(2,128)S(1)}, u32[]{:S(2)}, u32[]{:S(2)}) %collective-permute-start.1) | collective-permute-done | bytes 98336 | tf_op jit(solution)/shard_map/ppermute | solution.py:290
  12.2 0.1 pad_maximum_fusion
  12.3 2.1 %collective-permute-start.2 = (f32[4,3,2,2048]{3,2,1,0:T(2,128)S(1)}, f32[4,3,2,2048]{3,2,1,0:T(2,128)S(1)}, u32[]{:S(2)}, u32[]{:S(2)}) collective-permute-start(f32[4,3,2,2048]{3,2,1,0:T(2,128)S(1)} %pad_maximum_fusion), channel_id=1, source_target_pairs={{0,1},{1,0},{2,3},{3,2},{4,5},{5,4},{6,7},{7,6},{8,9},{9,8},{10,11... | collective-permute-start | bytes 589832 | tf_op jit(solution)/shard_map/ppermute | solution.py:290
  14.4 3.6 %density.6.refs_2_ = f32[2,256,128]{2,1,0:T(8,128)S(1)} custom-call(f32[2,3,2,2048]{3,2,1,0:T(2,128)S(1)} %collective-permute-done.1.refs_0_, f32[2,256,128]{2,1,0:T(8,128)S(1)} %density.5.refs_1_, f32[40,128]{1,0:T(8,128)S(1)} %get-tuple-element.23.refs_2_.refs_3_, s32[2,8]{1,0:T(2,128)S(1)} %get-tuple-element.24.refs_3_.refs_4_), custom_call_target="tpu_custom_call" | custom-call | flops 536870912 | bytes 98304 | tf_op jit(solution)/shard_map/density/pallas_call | solution.py:330
  17.9 0.3 %collective-permute-done.2.refs_1_ = f32[4,3,2,2048]{3,2,1,0:T(2,128)S(1)} collective-permute-done((f32[4,3,2,2048]{3,2,1,0:T(2,128)S(1)}, f32[4,3,2,2048]{3,2,1,0:T(2,128)S(1)}, u32[]{:S(2)}, u32[]{:S(2)}) %collective-permute-start.2) | collective-permute-done | bytes 196640 | tf_op jit(solution)/shard_map/ppermute | solution.py:290
  18.3 9.2 %density.7 = (f32[128,128]{1,0:T(8,128)S(1)}, f32[128,128]{1,0:T(8,128)S(1)}, f32[128,128]{1,0:T(8,128)S(1)}, f32[128,128]{1,0:T(8,128)S(1)}) custom-call(s32[128]{0:T(128)} %refs_0_.3, f32[4,3,2,2048]{3,2,1,0:T(2,128)S(1)} %collective-permute-done.2.refs_1_, f32[2,256,128]{2,1,0:T(8,128)S(1)} %density.6.refs_2_, ...), custom_call_target="tpu_custom_call" | custom-call | flops 1073741824 | bytes 196608 | tf_op jit(solution)/shard_map/density/pallas_call | solution.py:330
  27.5 0.1 collective-permute-start.3
  27.5 0.3 collective-permute-start.4
  27.8 1.6 %collective-permute-start.5 = (f32[128,128]{1,0:T(8,128)S(1)}, f32[128,128]{1,0:T(8,128)S(1)}, u32[]{:S(2)}, u32[]{:S(2)}) collective-permute-start(f32[128,128]{1,0:T(8,128)S(1)} %get-tuple-element.32), channel_id=1, source_target_pairs={{0,24},{8,16},{16,8},{24,0},{1,25},{9,17},{17,9},{25,1},{2,26},{10... | collective-permute-start | bytes 196616 | tf_op jit(solution)/shard_map/ppermute | solution.py:290
  29.4 0.0 collective-permute-done.3.refs_1_
  29.4 3.1 %collective-permute-done.4.refs_2_ = f32[128,128]{1,0:T(8,128)S(1)} collective-permute-done((f32[128,128]{1,0:T(8,128)S(1)}, f32[128,128]{1,0:T(8,128)S(1)}, u32[]{:S(2)}, u32[]{:S(2)}) %collective-permute-start.4) | collective-permute-done | bytes 65568 | tf_op jit(solution)/shard_map/ppermute | solution.py:290
  32.5 0.5 %collective-permute-done.5.refs_3_ = f32[128,128]{1,0:T(8,128)S(1)} collective-permute-done((f32[128,128]{1,0:T(8,128)S(1)}, f32[128,128]{1,0:T(8,128)S(1)}, u32[]{:S(2)}, u32[]{:S(2)}) %collective-permute-start.5) | collective-permute-done | bytes 65568 | tf_op jit(solution)/shard_map/ppermute | solution.py:290
  33.0 1.7 %spectrum.1 = f32[16,32,8,128]{3,2,1,0:T(8,128)} custom-call(f32[128,128]{1,0:T(8,128)S(1)} %get-tuple-element.29.refs_0_, f32[128,128]{1,0:T(8,128)S(1)} %collective-permute-done.3.refs_1_, f32[128,128]{1,0:T(8,128)S(1)} %collective-permute-done.4.refs_2_, f32[128,128]{1,0:T(8,128)S(1)} %collective-permute-done.5.refs_3_), custom_call_target="tpu_custom_call" | custom-call | tf_op jit(solution)/shard_map/spectrum/pallas_call | solution.py:364
  (1 shorter events, 0.0 us)
Async XLA Ops:
  0.0 7.4 %collective-permute-start = (f32[1,3,2,2048]{3,2,1,0:T(2,128)}, f32[1,3,2,2048]{3,2,1,0:T(2,128)S(1)}, u32[]{:S(2)}, u32[]{:S(2)}) collective-permute-start(f32[1,3,2,2048]{3,2,1,0:T(2,128)} %bitcast.1), channel_id=1, source_target_pairs={{0,4},{1,5},{2,6},{3,7},{4,0},{5,1},{6,2},{7,3},{8,12},{9,13},{10,... | collective-permute-start | bytes 147464 | tf_op jit(solution)/shard_map/ppermute | solution.py:290
  7.5 4.7 %collective-permute-start.1 = (f32[2,3,2,2048]{3,2,1,0:T(2,128)S(1)}, f32[2,3,2,2048]{3,2,1,0:T(2,128)S(1)}, u32[]{:S(2)}, u32[]{:S(2)}) collective-permute-start(f32[2,3,2,2048]{3,2,1,0:T(2,128)S(1)} %pad_maximum_fusion.1), channel_id=1, source_target_pairs={{0,2},{1,3},{2,0},{3,1},{4,6},{5,7},{6,4},{7,5},{8,10},{9,11},{10,... | collective-permute-start | bytes 294920 | tf_op jit(solution)/shard_map/ppermute | solution.py:290
  12.3 6.0 %collective-permute-start.2 = (f32[4,3,2,2048]{3,2,1,0:T(2,128)S(1)}, f32[4,3,2,2048]{3,2,1,0:T(2,128)S(1)}, u32[]{:S(2)}, u32[]{:S(2)}) collective-permute-start(f32[4,3,2,2048]{3,2,1,0:T(2,128)S(1)} %pad_maximum_fusion), channel_id=1, source_target_pairs={{0,1},{1,0},{2,3},{3,2},{4,5},{5,4},{6,7},{7,6},{8,9},{9,8},{10,11... | collective-permute-start | bytes 589832 | tf_op jit(solution)/shard_map/ppermute | solution.py:290
  27.5 1.9 %collective-permute-start.3 = (f32[128,128]{1,0:T(8,128)S(1)}, f32[128,128]{1,0:T(8,128)S(1)}, u32[]{:S(2)}, u32[]{:S(2)}) collective-permute-start(f32[128,128]{1,0:T(8,128)S(1)} %get-tuple-element.30), channel_id=1, source_target_pairs={{0,8},{8,0},{16,24},{24,16},{1,9},{9,1},{17,25},{25,17},{2,10},{10... | collective-permute-start | bytes 196616 | tf_op jit(solution)/shard_map/ppermute | solution.py:290
  27.5 5.0 %collective-permute-start.4 = (f32[128,128]{1,0:T(8,128)S(1)}, f32[128,128]{1,0:T(8,128)S(1)}, u32[]{:S(2)}, u32[]{:S(2)}) collective-permute-start(f32[128,128]{1,0:T(8,128)S(1)} %get-tuple-element.31), channel_id=1, source_target_pairs={{0,16},{8,24},{16,0},{24,8},{1,17},{9,25},{17,1},{25,9},{2,18},{10... | collective-permute-start | bytes 196616 | tf_op jit(solution)/shard_map/ppermute | solution.py:290
  27.8 5.2 %collective-permute-start.5 = (f32[128,128]{1,0:T(8,128)S(1)}, f32[128,128]{1,0:T(8,128)S(1)}, u32[]{:S(2)}, u32[]{:S(2)}) collective-permute-start(f32[128,128]{1,0:T(8,128)S(1)} %get-tuple-element.32), channel_id=1, source_target_pairs={{0,24},{8,16},{16,8},{24,0},{1,25},{9,17},{17,9},{25,1},{2,26},{10... | collective-permute-start | bytes 196616 | tf_op jit(solution)/shard_map/ppermute | solution.py:290

commit v4 on v3

--- a/solution.py
+++ b/solution.py
@@ -41,7 +41,7 @@
     return 1.0 - half_s * half_s, half_s * half_c
 
 
-def density_kernel(unit, ids, first, last, groups, n_x, n_z, share, *refs):
+def density_kernel(unit, frame_ids, ids, first, last, groups, n_x, n_z, share, *refs):
     n_args = 4 if first else 1 if last else 0
     args, refs = refs[:n_args], refs[n_args:]
     left_ref, right_ref, row_ref, arg_sem = refs[-4:]
@@ -83,7 +83,7 @@
             kb_ref[row : row + 1, :] = jnp.full((1, LANES), k, jnp.float32)
         copies[3].wait()
 
-    for frame in range(frames_here):
+    for frame in frame_ids:
         counts = [counts_ref[frame, brick ^ d] for d in ids]
         starts = [jnp.int32(0)]
         for count in counts:
@@ -177,10 +177,10 @@
 
     if last:
         copies[0].wait()
-        send_own_rows(outs, groups, rows, share, frames_here, local[0])
-
-
-def send_own_rows(outs, groups, rows, share, frames_here, ky_ref):
+        send_own_rows(outs, groups, rows, share, frame_ids, local[0])
+
+
+def send_own_rows(outs, groups, rows, share, frame_ids, ky_ref):
     prods = outs[-1]
     width = groups * share
     group = lax.axis_index("frames")
@@ -201,7 +201,7 @@
     )
     hot = jnp.concatenate([hot, hot, hot], axis=0)
     first_half = lax.broadcasted_iota(jnp.int32, (rows, 2 * KMAX), 1) < KMAX
-    for frame in range(frames_here):
+    for place, frame in enumerate(frame_ids):
         top = prods[frame, 0:rows, :]
         low = pltpu.roll(prods[frame, rows : 2 * rows, :], KMAX, 1)
         terms = jnp.where(first_half, top - low, -(top + low))
@@ -216,7 +216,7 @@
         for part in range(2):
             for dest in range(groups):
                 at = part * width + dest * share
-                to = (frame * 2 + part) * share
+                to = (place * 2 + part) * share
                 outs[dest][to : to + share, :] = picked[at : at + share, :]
 
 
@@ -242,15 +242,16 @@
         table_ref[at + size : at + 2 * size, :] = jnp.concatenate([none, part], axis=1)
 
 
-def spectrum_kernel(groups, share, chunk, n_x, n_z, frames_total, atoms, *refs):
-    srcs = refs[:groups]
-    out_hbm, out_ref, all_ref, table_ref, sem = refs[groups:]
+def spectrum_kernel(groups, frames_here, share, chunk, n_x, n_z, frames_total, atoms, *refs):
+    srcs = refs[: groups * frames_here]
+    out_hbm, out_ref, all_ref, table_ref, sem = refs[groups * frames_here :]
     block = srcs[0].shape[0]
-    terms = groups * block // share
+    terms = frames_total * 2
     rows = n_x * n_z
-    for distance in range(groups):
-        at = pl.multiple_of((lax.axis_index("frames") ^ distance) * block, block)
-        all_ref[pl.ds(at, block), :] = srcs[distance][...]
+    for frame in range(frames_here):
+        for distance in range(groups):
+            at = ((lax.axis_index("frames") ^ distance) * frames_here + frame) * block
+            all_ref[pl.ds(pl.multiple_of(at, block), block), :] = srcs[frame * groups + distance][...]
     dft_table(table_ref, frames_total, atoms)
 
     copies = []
@@ -297,14 +298,14 @@
     n_x, n_z = kvec_x.shape[0] // bricks, kvec_z.shape[0]
     rows = n_x * n_z
     share = kvec_y.shape[0] // groups
-    block = frames_here * 2 * share
+    block = 2 * share
     vmem = pl.BlockSpec(memory_space=pltpu.VMEM)
     prods_shape = (frames_here, 2 * rows, 2 * KMAX)
     waves_shape = (n_x + n_z + 16, LANES)
     hbm = pl.BlockSpec(memory_space=pltpu.HBM)
     smem = pl.BlockSpec(memory_space=pltpu.SMEM)
 
-    def density(shards, ids, sums, last):
+    def density(shards, ids, sums, last, frame_ids=tuple(range(positions.shape[1]))):
         first = sums is None
         unit = UNIT if len(ids) > 2 else UNIT // 2
         lanes = -(-len(ids) * capacity // (BIG * unit * LANES)) * BIG * unit * LANES
@@ -314,7 +315,7 @@
         scratch += [
             pltpu.VMEM((2 * rows, lanes), jnp.bfloat16),
             pltpu.VMEM((2 * KMAX, lanes), jnp.bfloat16),
-            pltpu.VMEM((unit * 2 * (n_x + 8), LANES), jnp.float32),
+            pltpu.VMEM((unit * 2 * (n_x + 8) + 8, LANES), jnp.float32),
             pltpu.SemaphoreType.DMA((4,)),
         ]
         if last:
@@ -326,9 +327,9 @@
                 out_shape.append(jax.ShapeDtypeStruct(waves_shape, jnp.float32))
                 out_shape.append(jax.ShapeDtypeStruct(counts.shape, jnp.int32))
                 out_shape.append(jax.ShapeDtypeStruct(shards.shape, jnp.float32))
-        atoms = frames_here * len(ids) * capacity
+        atoms = len(frame_ids) * len(ids) * capacity
         return pl.pallas_call(
-            functools.partial(density_kernel, unit, ids, first, last, groups, n_x, n_z, share),
+            functools.partial(density_kernel, unit, frame_ids, ids, first, last, groups, n_x, n_z, share),
             out_shape=out_shape,
             in_specs=[hbm] * len(args) + ([] if first else [vmem] * 3 + [smem]),
             out_specs=[vmem, vmem, smem, vmem] if first else [vmem] * len(out_shape),
@@ -355,28 +356,31 @@
         distance //= 2
         if distance:
             held = jnp.concatenate([held, got], axis=0)
-    sends = density(fresh, new, sums, True)
-    far = [swap(sends[d], "frames", groups, d) for d in range(groups - 1, 0, -1)]
-    got = [sends[0]] + far[::-1]
+    arrived = []
+    for frame in range(frames_here):
+        sends = density(got, new, sums, True, (frame,))
+        got, sends, arrived = lax.optimization_barrier((got, sends, arrived))
+        far = [swap(sends[d], "frames", groups, d) for d in range(1, groups)]
+        arrived += [sends[0]] + far
 
     chunk = min(8, share)
     frames_total = frames_here * groups
     return pl.pallas_call(
         functools.partial(
-            spectrum_kernel, groups, share, chunk, n_x, n_z, frames_total, capacity * bricks
+            spectrum_kernel, groups, frames_here, share, chunk, n_x, n_z, frames_total, capacity * bricks
         ),
         out_shape=jax.ShapeDtypeStruct((n_x, share, n_z, NW), jnp.float32),
-        in_specs=[vmem] * groups,
+        in_specs=[vmem] * len(arrived),
         out_specs=hbm,
         scratch_shapes=[
             pltpu.VMEM((n_x, share, n_z, NW), jnp.float32),
-            pltpu.VMEM((groups * block, rows), jnp.float32),
+            pltpu.VMEM((frames_total * block, rows), jnp.float32),
             pltpu.VMEM((12 * frames_total, 4 * NW), jnp.bfloat16),
             pltpu.SemaphoreType.DMA((share // chunk,)),
         ],
         compiler_params=pltpu.CompilerParams(vmem_limit_bytes=16 << 20),
         name="spectrum",
-    )(*got)
+    )(*arrived)
 
 
 def solution(mesh):

time: 34.6 us -> 37.6 us (1.087)
  starting transfers between devices: 9.27 us -> 13.9 us
  Pallas kernels: 20.9 us -> 20.1 us
  waiting for transfers between devices: 4.34 us -> 3.71 us
    ppermute x6 -> x9, starting transfers between devices: 9.27 us -> 13.9 us  [swap(): return lax.ppermute(value, axis, [(i, i ^ distance) for i in range(size)])]
    pallas_call x5 -> x6, Pallas kernels: 20.9 us -> 20.1 us  [the longest x5 18.4 us: density(): pl.pallas_call(functools.partial(density_kernel, unit, frame_ids, ids, fi...]
    ppermute x6 -> x9, waiting for transfers between devices: 4.34 us -> 3.71 us  [swap(): return lax.ppermute(value, axis, [(i, i ^ distance) for i in range(size)])]
  transfers between devices with their start and end apart: 6 -> 9, of which waited for: 4 -> 4; matrix products, arithmetic and copies ran while one was open for 0% -> 0% of each run, Pallas kernels for 29% -> 37%
where the time goes in v4:
time: 37.6 us; the launch traced here: 38.1 us
  Pallas kernels  20.1 us (53%)
  starting transfers between devices  13.9 us (37%)
  waiting for transfers between devices  3.71 us (10%)
    pallas_call x5, Pallas kernels, density(): pl.pallas_call(functools.partial(density_kernel, unit, frame_ids, ids, fi...  18.4 us
    ppermute x9, starting transfers between devices, swap(): return lax.ppermute(value, axis, [(i, i ^ distance) for i in range(size)])  13.9 us
    ppermute x9, waiting for transfers between devices, swap(): return lax.ppermute(value, axis, [(i, i ^ distance) for i in range(size)])  3.71 us
    pallas_call x1, Pallas kernels, per_device(): pl.pallas_call(functools.partial(spectrum_kernel, groups, frames_here, sh...  1.71 us
  transfers between devices with their start and end apart: 9, of which 4 were waited for; matrix products, arithmetic and copies ran while one was open for 0% of the time, Pallas kernels for 37%

profile of v4, /device:TPU:0, one launch (start us, length us, event | category | flops | bytes accessed | tf_op | source)
XLA Modules:
  0.0 38.1 jit_solution(15966028970438059962)
XLA Ops:
  0.0 4.0 %collective-permute-start = (f32[1,3,2,2048]{3,2,1,0:T(2,128)}, f32[1,3,2,2048]{3,2,1,0:T(2,128)S(1)}, u32[]{:S(2)}, u32[]{:S(2)}) collective-permute-start(f32[1,3,2,2048]{3,2,1,0:T(2,128)} %bitcast.1), channel_id=1, source_target_pairs={{0,4},{1,5},{2,6},{3,7},{4,0},{5,1},{6,2},{7,3},{8,12},{9,13},{10,... | collective-permute-start | bytes 147464 | tf_op jit(solution)/shard_map/ppermute | solution.py:291
  4.0 3.1 %density.5 = (f32[2,256,128]{2,1,0:T(8,128)S(1)}, f32[40,128]{1,0:T(8,128)S(1)}, s32[2,8]{1,0:T(2,128)S(1)}, f32[1,3,2,2048]{3,2,1,0:T(2,128)S(1)}) custom-call(s32[2,8]{1,0:T(2,128)} %refs_0_.3, s32[128]{0:T(128)} %refs_1_.1, s32[8]{0:T(128)} %refs_2_.1, f32[1,3,2,2048]{3,2,1,0:T(2,128)} %bitcast.2), custom_call_target="tpu_custom_call" | custom-call | flops 268435456 | bytes 49152 | tf_op jit(solution)/shard_map/density/pallas_call | solution.py:331
  7.2 0.0 collective-permute-done.refs_0_
  7.2 1.9 %collective-permute-start.1 = (f32[2,3,2,2048]{3,2,1,0:T(2,128)S(1)}, f32[2,3,2,2048]{3,2,1,0:T(2,128)S(1)}, u32[]{:S(2)}, u32[]{:S(2)}) collective-permute-start(f32[2,3,2,2048]{3,2,1,0:T(2,128)S(1)} %pad_maximum_fusion.1), channel_id=1, source_target_pairs={{0,2},{1,3},{2,0},{3,1},{4,6},{5,7},{6,4},{7,5},{8,10},{9,11},{10,... | collective-permute-start | bytes 294920 | tf_op jit(solution)/shard_map/ppermute | solution.py:291
  9.1 2.5 %density.6.refs_1_ = f32[2,256,128]{2,1,0:T(8,128)S(1)} custom-call(f32[1,3,2,2048]{3,2,1,0:T(2,128)S(1)} %collective-permute-done.refs_0_, f32[2,256,128]{2,1,0:T(8,128)S(1)} %get-tuple-element.39.refs_1_, f32[40,128]{1,0:T(8,128)S(1)} %get-tuple-element.40.refs_2_.refs_3_, s32[2,8]{1,0:T(2,128)S(1)} %get-tuple-element.41.refs_3_.refs_4_), custom_call_target="tpu_custom_call" | custom-call | flops 268435456 | bytes 49152 | tf_op jit(solution)/shard_map/density/pallas_call | solution.py:331
  11.7 0.2 collective-permute-done.1.refs_0_
  11.9 0.1 pad_maximum_fusion
  12.0 2.0 %collective-permute-start.2 = (f32[4,3,2,2048]{3,2,1,0:T(2,128)S(1)}, f32[4,3,2,2048]{3,2,1,0:T(2,128)S(1)}, u32[]{:S(2)}, u32[]{:S(2)}) collective-permute-start(f32[4,3,2,2048]{3,2,1,0:T(2,128)S(1)} %pad_maximum_fusion), channel_id=1, source_target_pairs={{0,1},{1,0},{2,3},{3,2},{4,5},{5,4},{6,7},{7,6},{8,9},{9,8},{10,11... | collective-permute-start | bytes 589832 | tf_op jit(solution)/shard_map/ppermute | solution.py:291
  14.0 4.5 %density.7.refs_2_ = f32[2,256,128]{2,1,0:T(8,128)S(1)} custom-call(f32[2,3,2,2048]{3,2,1,0:T(2,128)S(1)} %collective-permute-done.1.refs_0_, f32[2,256,128]{2,1,0:T(8,128)S(1)} %density.6.refs_1_, f32[40,128]{1,0:T(8,128)S(1)} %get-tuple-element.40.refs_2_.refs_3_, s32[2,8]{1,0:T(2,128)S(1)} %get-tuple-element.41.refs_3_.refs_4_), custom_call_target="tpu_custom_call" | custom-call | flops 536870912 | bytes 98304 | tf_op jit(solution)/shard_map/density/pallas_call | solution.py:331
  18.6 0.2 collective-permute-done.2.refs_1_
  18.8 4.5 %density.8 = (f32[64,128]{1,0:T(8,128)S(1)}, f32[64,128]{1,0:T(8,128)S(1)}, f32[64,128]{1,0:T(8,128)S(1)}, f32[64,128]{1,0:T(8,128)S(1)}) custom-call(s32[128]{0:T(128)} %refs_0_.5, f32[4,3,2,2048]{3,2,1,0:T(2,128)S(1)} %collective-permute-done.2.refs_1_, f32[2,256,128]{2,1,0:T(8,128)S(1)} %density.7.refs_2_, ...), custom_call_target="tpu_custom_call" | custom-call | flops 536870912 | bytes 98304 | tf_op jit(solution)/shard_map/density/pallas_call | solution.py:331
  23.2 0.1 collective-permute-start.3
  23.3 2.7 %collective-permute-start.4 = (f32[64,128]{1,0:T(8,128)S(1)}, f32[64,128]{1,0:T(8,128)S(1)}, u32[]{:S(2)}, u32[]{:S(2)}) collective-permute-start(f32[64,128]{1,0:T(8,128)S(1)} %get-tuple-element.57), channel_id=1, source_target_pairs={{0,16},{8,24},{16,0},{24,8},{1,17},{9,25},{17,1},{25,9},{2,18},{10... | collective-permute-start | bytes 98312 | tf_op jit(solution)/shard_map/ppermute | solution.py:291
  26.1 0.1 collective-permute-start.5
  26.1 3.7 %density.9 = (f32[64,128]{1,0:T(8,128)S(1)}, f32[64,128]{1,0:T(8,128)S(1)}, f32[64,128]{1,0:T(8,128)S(1)}, f32[64,128]{1,0:T(8,128)S(1)}) custom-call(s32[128]{0:T(128)} %refs_0_.5, f32[4,3,2,2048]{3,2,1,0:T(2,128)S(1)} %collective-permute-done.2.refs_1_, f32[2,256,128]{2,1,0:T(8,128)S(1)} %density.7.refs_2_, ...), custom_call_target="tpu_custom_call" | custom-call | flops 536870912 | bytes 98304 | tf_op jit(solution)/shard_map/density/pallas_call | solution.py:331
  29.9 0.0 collective-permute-done.3.refs_1_
  29.9 0.0 collective-permute-done.4.refs_2_
  29.9 0.0 collective-permute-done.5.refs_3_
  29.9 0.7 %collective-permute-start.6 = (f32[64,128]{1,0:T(8,128)S(1)}, f32[64,128]{1,0:T(8,128)S(1)}, u32[]{:S(2)}, u32[]{:S(2)}) collective-permute-start(f32[64,128]{1,0:T(8,128)S(1)} %get-tuple-element.64), channel_id=1, source_target_pairs={{0,8},{8,0},{16,24},{24,16},{1,9},{9,1},{17,25},{25,17},{2,10},{10... | collective-permute-start | bytes 98312 | tf_op jit(solution)/shard_map/ppermute | solution.py:291
  30.7 2.2 %collective-permute-start.7 = (f32[64,128]{1,0:T(8,128)S(1)}, f32[64,128]{1,0:T(8,128)S(1)}, u32[]{:S(2)}, u32[]{:S(2)}) collective-permute-start(f32[64,128]{1,0:T(8,128)S(1)} %get-tuple-element.65), channel_id=1, source_target_pairs={{0,16},{8,24},{16,0},{24,8},{1,17},{9,25},{17,1},{25,9},{2,18},{10... | collective-permute-start | bytes 98312 | tf_op jit(solution)/shard_map/ppermute | solution.py:291
  32.9 0.1 collective-permute-start.8
  32.9 0.0 collective-permute-done.6.refs_5_
  32.9 1.9 %collective-permute-done.7.refs_6_ = f32[64,128]{1,0:T(8,128)S(1)} collective-permute-done((f32[64,128]{1,0:T(8,128)S(1)}, f32[64,128]{1,0:T(8,128)S(1)}, u32[]{:S(2)}, u32[]{:S(2)}) %collective-permute-start.7) | collective-permute-done | bytes 32800 | tf_op jit(solution)/shard_map/ppermute | solution.py:291
  34.8 1.4 %collective-permute-done.8.refs_7_ = f32[64,128]{1,0:T(8,128)S(1)} collective-permute-done((f32[64,128]{1,0:T(8,128)S(1)}, f32[64,128]{1,0:T(8,128)S(1)}, u32[]{:S(2)}, u32[]{:S(2)}) %collective-permute-start.8) | collective-permute-done | bytes 32800 | tf_op jit(solution)/shard_map/ppermute | solution.py:291
  36.2 1.7 %spectrum.1 = f32[16,32,8,128]{3,2,1,0:T(8,128)} custom-call(f32[64,128]{1,0:T(8,128)S(1)} %get-tuple-element.59.refs_0_, f32[64,128]{1,0:T(8,128)S(1)} %collective-permute-done.3.refs_1_, f32[64,128]{1,0:T(8,128)S(1)} %collective-permute-done.4.refs_2_, f32[64,128]{1,0:T(8,128)S(1)} %collective-permute-done.5.refs_3_, ...), custom_call_target="tpu_custom_call" | custom-call | tf_op jit(solution)/shard_map/spectrum/pallas_call | solution.py:368
  (1 shorter events, 0.0 us)
Async XLA Ops:
  0.0 7.2 %collective-permute-start = (f32[1,3,2,2048]{3,2,1,0:T(2,128)}, f32[1,3,2,2048]{3,2,1,0:T(2,128)S(1)}, u32[]{:S(2)}, u32[]{:S(2)}) collective-permute-start(f32[1,3,2,2048]{3,2,1,0:T(2,128)} %bitcast.1), channel_id=1, source_target_pairs={{0,4},{1,5},{2,6},{3,7},{4,0},{5,1},{6,2},{7,3},{8,12},{9,13},{10,... | collective-permute-start | bytes 147464 | tf_op jit(solution)/shard_map/ppermute | solution.py:291
  7.2 4.7 %collective-permute-start.1 = (f32[2,3,2,2048]{3,2,1,0:T(2,128)S(1)}, f32[2,3,2,2048]{3,2,1,0:T(2,128)S(1)}, u32[]{:S(2)}, u32[]{:S(2)}) collective-permute-start(f32[2,3,2,2048]{3,2,1,0:T(2,128)S(1)} %pad_maximum_fusion.1), channel_id=1, source_target_pairs={{0,2},{1,3},{2,0},{3,1},{4,6},{5,7},{6,4},{7,5},{8,10},{9,11},{10,... | collective-permute-start | bytes 294920 | tf_op jit(solution)/shard_map/ppermute | solution.py:291
  12.0 6.8 %collective-permute-start.2 = (f32[4,3,2,2048]{3,2,1,0:T(2,128)S(1)}, f32[4,3,2,2048]{3,2,1,0:T(2,128)S(1)}, u32[]{:S(2)}, u32[]{:S(2)}) collective-permute-start(f32[4,3,2,2048]{3,2,1,0:T(2,128)S(1)} %pad_maximum_fusion), channel_id=1, source_target_pairs={{0,1},{1,0},{2,3},{3,2},{4,5},{5,4},{6,7},{7,6},{8,9},{9,8},{10,11... | collective-permute-start | bytes 589832 | tf_op jit(solution)/shard_map/ppermute | solution.py:291
  23.2 6.6 %collective-permute-start.3 = (f32[64,128]{1,0:T(8,128)S(1)}, f32[64,128]{1,0:T(8,128)S(1)}, u32[]{:S(2)}, u32[]{:S(2)}) collective-permute-start(f32[64,128]{1,0:T(8,128)S(1)} %get-tuple-element.56), channel_id=1, source_target_pairs={{0,8},{8,0},{16,24},{24,16},{1,9},{9,1},{17,25},{25,17},{2,10},{10... | collective-permute-start | bytes 98312 | tf_op jit(solution)/shard_map/ppermute | solution.py:291
  23.3 6.6 %collective-permute-start.4 = (f32[64,128]{1,0:T(8,128)S(1)}, f32[64,128]{1,0:T(8,128)S(1)}, u32[]{:S(2)}, u32[]{:S(2)}) collective-permute-start(f32[64,128]{1,0:T(8,128)S(1)} %get-tuple-element.57), channel_id=1, source_target_pairs={{0,16},{8,24},{16,0},{24,8},{1,17},{9,25},{17,1},{25,9},{2,18},{10... | collective-permute-start | bytes 98312 | tf_op jit(solution)/shard_map/ppermute | solution.py:291
  26.1 3.8 %collective-permute-start.5 = (f32[64,128]{1,0:T(8,128)S(1)}, f32[64,128]{1,0:T(8,128)S(1)}, u32[]{:S(2)}, u32[]{:S(2)}) collective-permute-start(f32[64,128]{1,0:T(8,128)S(1)} %get-tuple-element.58), channel_id=1, source_target_pairs={{0,24},{8,16},{16,8},{24,0},{1,25},{9,17},{17,9},{25,1},{2,26},{10... | collective-permute-start | bytes 98312 | tf_op jit(solution)/shard_map/ppermute | solution.py:291
  29.9 3.0 %collective-permute-start.6 = (f32[64,128]{1,0:T(8,128)S(1)}, f32[64,128]{1,0:T(8,128)S(1)}, u32[]{:S(2)}, u32[]{:S(2)}) collective-permute-start(f32[64,128]{1,0:T(8,128)S(1)} %get-tuple-element.64), channel_id=1, source_target_pairs={{0,8},{8,0},{16,24},{24,16},{1,9},{9,1},{17,25},{25,17},{2,10},{10... | collective-permute-start | bytes 98312 | tf_op jit(solution)/shard_map/ppermute | solution.py:291
  30.7 4.2 %collective-permute-start.7 = (f32[64,128]{1,0:T(8,128)S(1)}, f32[64,128]{1,0:T(8,128)S(1)}, u32[]{:S(2)}, u32[]{:S(2)}) collective-permute-start(f32[64,128]{1,0:T(8,128)S(1)} %get-tuple-element.65), channel_id=1, source_target_pairs={{0,16},{8,24},{16,0},{24,8},{1,17},{9,25},{17,1},{25,9},{2,18},{10... | collective-permute-start | bytes 98312 | tf_op jit(solution)/shard_map/ppermute | solution.py:291
  32.9 3.3 %collective-permute-start.8 = (f32[64,128]{1,0:T(8,128)S(1)}, f32[64,128]{1,0:T(8,128)S(1)}, u32[]{:S(2)}, u32[]{:S(2)}) collective-permute-start(f32[64,128]{1,0:T(8,128)S(1)} %get-tuple-element.66), channel_id=1, source_target_pairs={{0,24},{8,16},{16,8},{24,0},{1,25},{9,17},{17,9},{25,1},{2,26},{10... | collective-permute-start | bytes 98312 | tf_op jit(solution)/shard_map/ppermute | solution.py:291

commit v5 on v3

--- a/solution.py
+++ b/solution.py
@@ -220,7 +220,7 @@
                 outs[dest][to : to + share, :] = picked[at : at + share, :]
 
 
-def dft_table(table_ref, frames_total, atoms):
+def dft_table(frames_total, atoms, after_ref, table_ref):
     weights = [0.5 - 0.5 * math.cos(2.0 * math.pi * (t + 0.5) / frames_total) for t in range(frames_total)]
     scale = 1.0 / math.sqrt(atoms * sum(w * w for w in weights))
     shape = (2 * frames_total, NW)
@@ -242,17 +242,15 @@
         table_ref[at + size : at + 2 * size, :] = jnp.concatenate([none, part], axis=1)
 
 
-def spectrum_kernel(groups, share, chunk, n_x, n_z, frames_total, atoms, *refs):
+def spectrum_kernel(groups, share, chunk, n_x, n_z, *refs):
     srcs = refs[:groups]
-    out_hbm, out_ref, all_ref, table_ref, sem = refs[groups:]
+    table_ref, out_hbm, out_ref, all_ref, sem = refs[groups:]
     block = srcs[0].shape[0]
     terms = groups * block // share
     rows = n_x * n_z
     for distance in range(groups):
         at = pl.multiple_of((lax.axis_index("frames") ^ distance) * block, block)
         all_ref[pl.ds(at, block), :] = srcs[distance][...]
-    dft_table(table_ref, frames_total, atoms)
-
     copies = []
     for base in range(0, share, chunk):
         for first in range(base, base + chunk, 2 * PAIRS):
@@ -314,7 +312,7 @@
         scratch += [
             pltpu.VMEM((2 * rows, lanes), jnp.bfloat16),
             pltpu.VMEM((2 * KMAX, lanes), jnp.bfloat16),
-            pltpu.VMEM((unit * 2 * (n_x + 8), LANES), jnp.float32),
+            pltpu.VMEM((unit * 2 * (n_x + 8) + 8, LANES), jnp.float32),
             pltpu.SemaphoreType.DMA((4,)),
         ]
         if last:
@@ -361,22 +359,27 @@
 
     chunk = min(8, share)
     frames_total = frames_here * groups
+    table = pl.pallas_call(
+        functools.partial(dft_table, frames_total, capacity * bricks),
+        out_shape=jax.ShapeDtypeStruct((12 * frames_total, 4 * NW), jnp.bfloat16),
+        in_specs=[pl.BlockSpec(memory_space=pl.ANY)],
+        out_specs=vmem,
+        compiler_params=pltpu.CompilerParams(vmem_limit_bytes=16 << 20),
+        name="table",
+    )(sends[0])
     return pl.pallas_call(
-        functools.partial(
-            spectrum_kernel, groups, share, chunk, n_x, n_z, frames_total, capacity * bricks
-        ),
+        functools.partial(spectrum_kernel, groups, share, chunk, n_x, n_z),
         out_shape=jax.ShapeDtypeStruct((n_x, share, n_z, NW), jnp.float32),
-        in_specs=[vmem] * groups,
+        in_specs=[vmem] * (groups + 1),
         out_specs=hbm,
         scratch_shapes=[
             pltpu.VMEM((n_x, share, n_z, NW), jnp.float32),
             pltpu.VMEM((groups * block, rows), jnp.float32),
-            pltpu.VMEM((12 * frames_total, 4 * NW), jnp.bfloat16),
             pltpu.SemaphoreType.DMA((share // chunk,)),
         ],
         compiler_params=pltpu.CompilerParams(vmem_limit_bytes=16 << 20),
         name="spectrum",
-    )(*got)
+    )(*got, table)
 
 
 def solution(mesh):

time: 34.6 us -> 34 us (0.983); the launches traced: 34.9 us -> 33.8 us
  Pallas kernels: 20.9 us -> 18.3 us
  waiting for transfers between devices: 4.34 us -> 5.83 us
    pallas_call x4, Pallas kernels: 19.2 us -> 16.6 us  [density(): pl.pallas_call(functools.partial(density_kernel, unit, ids, first, last,...]
    ppermute x6, waiting for transfers between devices: 4.34 us -> 5.83 us  [swap(): return lax.ppermute(value, axis, [(i, i ^ distance) for i in range(size)])]
  transfers between devices with their start and end apart: 6 -> 6, of which waited for: 4 -> 4; matrix products, arithmetic and copies ran while one was open for 0% -> 0% of each run, Pallas kernels for 29% -> 24%
where the time goes in v5:
time: 34 us; the launch traced here: 33.8 us
  Pallas kernels  18.3 us (54%)
  starting transfers between devices  9.26 us (27%)
  waiting for transfers between devices  5.83 us (17%)
    pallas_call x4, Pallas kernels, density(): pl.pallas_call(functools.partial(density_kernel, unit, ids, first, last,...  16.6 us
    ppermute x6, starting transfers between devices, swap(): return lax.ppermute(value, axis, [(i, i ^ distance) for i in range(size)])  9.26 us
    ppermute x6, waiting for transfers between devices, swap(): return lax.ppermute(value, axis, [(i, i ^ distance) for i in range(size)])  5.83 us
    pallas_call x1, Pallas kernels, per_device(): pl.pallas_call(functools.partial(spectrum_kernel, groups, share, chunk, n...  1.71 us
  transfers between devices with their start and end apart: 6, of which 4 were waited for; matrix products, arithmetic and copies ran while one was open for 0% of the time, Pallas kernels for 24%

profile of v5, /device:TPU:0, one launch (start us, length us, event | category | flops | bytes accessed | tf_op | source)
XLA Modules:
  0.0 33.8 jit_solution(4869668892285228799)
XLA Ops:
  0.0 4.0 %collective-permute-start = (f32[1,3,2,2048]{3,2,1,0:T(2,128)}, f32[1,3,2,2048]{3,2,1,0:T(2,128)S(1)}, u32[]{:S(2)}, u32[]{:S(2)}) collective-permute-start(f32[1,3,2,2048]{3,2,1,0:T(2,128)} %bitcast.1), channel_id=1, source_target_pairs={{0,4},{1,5},{2,6},{3,7},{4,0},{5,1},{6,2},{7,3},{8,12},{9,13},{10,... | collective-permute-start | bytes 147464 | tf_op jit(solution)/shard_map/ppermute | solution.py:288
  4.0 3.1 %density.4 = (f32[2,256,128]{2,1,0:T(8,128)S(1)}, f32[40,128]{1,0:T(8,128)S(1)}, s32[2,8]{1,0:T(2,128)S(1)}, f32[1,3,2,2048]{3,2,1,0:T(2,128)S(1)}) custom-call(s32[2,8]{1,0:T(2,128)} %refs_0_.2, s32[128]{0:T(128)} %refs_1_.1, s32[8]{0:T(128)} %refs_2_.1, f32[1,3,2,2048]{3,2,1,0:T(2,128)} %bitcast.2), custom_call_target="tpu_custom_call" | custom-call | flops 268435456 | bytes 49152 | tf_op jit(solution)/shard_map/density/pallas_call | solution.py:328
  7.2 0.0 collective-permute-done.refs_0_
  7.2 1.1 %collective-permute-start.1 = (f32[2,3,2,2048]{3,2,1,0:T(2,128)S(1)}, f32[2,3,2,2048]{3,2,1,0:T(2,128)S(1)}, u32[]{:S(2)}, u32[]{:S(2)}) collective-permute-start(f32[2,3,2,2048]{3,2,1,0:T(2,128)S(1)} %pad_maximum_fusion.1), channel_id=1, source_target_pairs={{0,2},{1,3},{2,0},{3,1},{4,6},{5,7},{6,4},{7,5},{8,10},{9,11},{10,... | collective-permute-start | bytes 294920 | tf_op jit(solution)/shard_map/ppermute | solution.py:288
  8.3 1.8 %density.5.refs_1_ = f32[2,256,128]{2,1,0:T(8,128)S(1)} custom-call(f32[1,3,2,2048]{3,2,1,0:T(2,128)S(1)} %collective-permute-done.refs_0_, f32[2,256,128]{2,1,0:T(8,128)S(1)} %get-tuple-element.22.refs_1_, f32[40,128]{1,0:T(8,128)S(1)} %get-tuple-element.23.refs_2_.refs_3_, s32[2,8]{1,0:T(2,128)S(1)} %get-tuple-element.24.refs_3_.refs_4_), custom_call_target="tpu_custom_call" | custom-call | flops 268435456 | bytes 49152 | tf_op jit(solution)/shard_map/density/pallas_call | solution.py:328
  10.2 1.8 %collective-permute-done.1.refs_0_ = f32[2,3,2,2048]{3,2,1,0:T(2,128)S(1)} collective-permute-done((f32[2,3,2,2048]{3,2,1,0:T(2,128)S(1)}, f32[2,3,2,2048]{3,2,1,0:T(2,128)S(1)}, u32[]{:S(2)}, u32[]{:S(2)}) %collective-permute-start.1) | collective-permute-done | bytes 98336 | tf_op jit(solution)/shard_map/ppermute | solution.py:288
  12.0 0.1 pad_maximum_fusion
  12.1 2.2 %collective-permute-start.2 = (f32[4,3,2,2048]{3,2,1,0:T(2,128)S(1)}, f32[4,3,2,2048]{3,2,1,0:T(2,128)S(1)}, u32[]{:S(2)}, u32[]{:S(2)}) collective-permute-start(f32[4,3,2,2048]{3,2,1,0:T(2,128)S(1)} %pad_maximum_fusion), channel_id=1, source_target_pairs={{0,1},{1,0},{2,3},{3,2},{4,5},{5,4},{6,7},{7,6},{8,9},{9,8},{10,11... | collective-permute-start | bytes 589832 | tf_op jit(solution)/shard_map/ppermute | solution.py:288
  14.2 3.3 %density.6.refs_2_ = f32[2,256,128]{2,1,0:T(8,128)S(1)} custom-call(f32[2,3,2,2048]{3,2,1,0:T(2,128)S(1)} %collective-permute-done.1.refs_0_, f32[2,256,128]{2,1,0:T(8,128)S(1)} %density.5.refs_1_, f32[40,128]{1,0:T(8,128)S(1)} %get-tuple-element.23.refs_2_.refs_3_, s32[2,8]{1,0:T(2,128)S(1)} %get-tuple-element.24.refs_3_.refs_4_), custom_call_target="tpu_custom_call" | custom-call | flops 536870912 | bytes 98304 | tf_op jit(solution)/shard_map/density/pallas_call | solution.py:328
  17.5 0.5 %collective-permute-done.2.refs_1_ = f32[4,3,2,2048]{3,2,1,0:T(2,128)S(1)} collective-permute-done((f32[4,3,2,2048]{3,2,1,0:T(2,128)S(1)}, f32[4,3,2,2048]{3,2,1,0:T(2,128)S(1)}, u32[]{:S(2)}, u32[]{:S(2)}) %collective-permute-start.2) | collective-permute-done | bytes 196640 | tf_op jit(solution)/shard_map/ppermute | solution.py:288
  18.0 8.4 %density.7 = (f32[128,128]{1,0:T(8,128)S(1)}, f32[128,128]{1,0:T(8,128)S(1)}, f32[128,128]{1,0:T(8,128)S(1)}, f32[128,128]{1,0:T(8,128)S(1)}) custom-call(s32[128]{0:T(128)} %refs_0_.3, f32[4,3,2,2048]{3,2,1,0:T(2,128)S(1)} %collective-permute-done.2.refs_1_, f32[2,256,128]{2,1,0:T(8,128)S(1)} %density.6.refs_2_, ...), custom_call_target="tpu_custom_call" | custom-call | flops 1073741824 | bytes 196608 | tf_op jit(solution)/shard_map/density/pallas_call | solution.py:328
  26.4 0.1 collective-permute-start.3
  26.5 0.1 collective-permute-start.4
  26.6 1.8 %collective-permute-start.5 = (f32[128,128]{1,0:T(8,128)S(1)}, f32[128,128]{1,0:T(8,128)S(1)}, u32[]{:S(2)}, u32[]{:S(2)}) collective-permute-start(f32[128,128]{1,0:T(8,128)S(1)} %get-tuple-element.32), channel_id=1, source_target_pairs={{0,24},{8,16},{16,8},{24,0},{1,25},{9,17},{17,9},{25,1},{2,26},{10... | collective-permute-start | bytes 196616 | tf_op jit(solution)/shard_map/ppermute | solution.py:288
  28.4 0.0 collective-permute-done.3.refs_1_
  28.4 3.0 %collective-permute-done.4.refs_2_ = f32[128,128]{1,0:T(8,128)S(1)} collective-permute-done((f32[128,128]{1,0:T(8,128)S(1)}, f32[128,128]{1,0:T(8,128)S(1)}, u32[]{:S(2)}, u32[]{:S(2)}) %collective-permute-start.4) | collective-permute-done | bytes 65568 | tf_op jit(solution)/shard_map/ppermute | solution.py:288
  31.4 0.5 %collective-permute-done.5.refs_3_ = f32[128,128]{1,0:T(8,128)S(1)} collective-permute-done((f32[128,128]{1,0:T(8,128)S(1)}, f32[128,128]{1,0:T(8,128)S(1)}, u32[]{:S(2)}, u32[]{:S(2)}) %collective-permute-start.5) | collective-permute-done | bytes 65568 | tf_op jit(solution)/shard_map/ppermute | solution.py:288
  31.9 1.7 %spectrum.1 = f32[16,32,8,128]{3,2,1,0:T(8,128)} custom-call(f32[128,128]{1,0:T(8,128)S(1)} %get-tuple-element.29.after_ref.refs_0_, f32[128,128]{1,0:T(8,128)S(1)} %collective-permute-done.3.refs_1_, f32[128,128]{1,0:T(8,128)S(1)} %collective-permute-done.4.refs_2_, f32[128,128]{1,0:T(8,128)S(1)} %collective-permute-done.5.refs_3_, ...), custom_call_target="tpu_custom_call" | custom-call | tf_op jit(solution)/shard_map/spectrum/pallas_call | solution.py:370
  (2 shorter events, 0.1 us)
Async XLA Ops:
  0.0 7.2 %collective-permute-start = (f32[1,3,2,2048]{3,2,1,0:T(2,128)}, f32[1,3,2,2048]{3,2,1,0:T(2,128)S(1)}, u32[]{:S(2)}, u32[]{:S(2)}) collective-permute-start(f32[1,3,2,2048]{3,2,1,0:T(2,128)} %bitcast.1), channel_id=1, source_target_pairs={{0,4},{1,5},{2,6},{3,7},{4,0},{5,1},{6,2},{7,3},{8,12},{9,13},{10,... | collective-permute-start | bytes 147464 | tf_op jit(solution)/shard_map/ppermute | solution.py:288
  7.2 4.7 %collective-permute-start.1 = (f32[2,3,2,2048]{3,2,1,0:T(2,128)S(1)}, f32[2,3,2,2048]{3,2,1,0:T(2,128)S(1)}, u32[]{:S(2)}, u32[]{:S(2)}) collective-permute-start(f32[2,3,2,2048]{3,2,1,0:T(2,128)S(1)} %pad_maximum_fusion.1), channel_id=1, source_target_pairs={{0,2},{1,3},{2,0},{3,1},{4,6},{5,7},{6,4},{7,5},{8,10},{9,11},{10,... | collective-permute-start | bytes 294920 | tf_op jit(solution)/shard_map/ppermute | solution.py:288
  12.1 6.0 %collective-permute-start.2 = (f32[4,3,2,2048]{3,2,1,0:T(2,128)S(1)}, f32[4,3,2,2048]{3,2,1,0:T(2,128)S(1)}, u32[]{:S(2)}, u32[]{:S(2)}) collective-permute-start(f32[4,3,2,2048]{3,2,1,0:T(2,128)S(1)} %pad_maximum_fusion), channel_id=1, source_target_pairs={{0,1},{1,0},{2,3},{3,2},{4,5},{5,4},{6,7},{7,6},{8,9},{9,8},{10,11... | collective-permute-start | bytes 589832 | tf_op jit(solution)/shard_map/ppermute | solution.py:288
  26.4 2.0 %collective-permute-start.3 = (f32[128,128]{1,0:T(8,128)S(1)}, f32[128,128]{1,0:T(8,128)S(1)}, u32[]{:S(2)}, u32[]{:S(2)}) collective-permute-start(f32[128,128]{1,0:T(8,128)S(1)} %get-tuple-element.30), channel_id=1, source_target_pairs={{0,8},{8,0},{16,24},{24,16},{1,9},{9,1},{17,25},{25,17},{2,10},{10... | collective-permute-start | bytes 196616 | tf_op jit(solution)/shard_map/ppermute | solution.py:288
  26.5 5.0 %collective-permute-start.4 = (f32[128,128]{1,0:T(8,128)S(1)}, f32[128,128]{1,0:T(8,128)S(1)}, u32[]{:S(2)}, u32[]{:S(2)}) collective-permute-start(f32[128,128]{1,0:T(8,128)S(1)} %get-tuple-element.31), channel_id=1, source_target_pairs={{0,16},{8,24},{16,0},{24,8},{1,17},{9,25},{17,1},{25,9},{2,18},{10... | collective-permute-start | bytes 196616 | tf_op jit(solution)/shard_map/ppermute | solution.py:288
  26.6 5.4 %collective-permute-start.5 = (f32[128,128]{1,0:T(8,128)S(1)}, f32[128,128]{1,0:T(8,128)S(1)}, u32[]{:S(2)}, u32[]{:S(2)}) collective-permute-start(f32[128,128]{1,0:T(8,128)S(1)} %get-tuple-element.32), channel_id=1, source_target_pairs={{0,24},{8,16},{16,8},{24,0},{1,25},{9,17},{17,9},{25,1},{2,26},{10... | collective-permute-start | bytes 196616 | tf_op jit(solution)/shard_map/ppermute | solution.py:288
